TPU v7x, 32 devices: a whole 2x2x4 slice. The times are simulated.
32 devices in a mesh: shard: 16 (over z, y, x), replica: 2 (over core).
Axes of the slice: x: 2, y: 2, z: 4, core: 2. Of those that a mesh axis runs over, the one named last changes fastest.
Arguments:
- latents: bfloat16 [8192, 1280], P(('shard', 'replica')), may hold values from -6 to 6
- noise: bfloat16 [8192, 1280], P(('shard', 'replica')), may hold values from -6 to 6
- timesteps: int32 [16], replicated, may hold values from 0 to 999
- master_weight: float32 [1280, 1280], P('shard'), may hold values from -0.15625 to 0.15625
- norm_gain: float32 [1280], P('shard'), may hold values from 0.5 to 1.5
- weight_moment: float32 [1280, 1280], P('shard'), may hold values from -4 to 4
- weight_second: float32 [1280, 1280], P('shard'), may hold values from 0.1 to 2
- gain_moment: float32 [1280], P('shard'), may hold values from -4 to 4
- gain_second: float32 [1280], P('shard'), may hold values from 0.1 to 2
Outputs:
- new_weight: float32 [1280, 1280], P('shard')
- new_weight_moment: float32 [1280, 1280], P('shard')
- new_weight_second: float32 [1280, 1280], P('shard')
- new_gain: float32 [1280], P('shard')
- new_gain_moment: float32 [1280], P('shard')
- new_gain_second: float32 [1280], P('shard')
All inputs are finite; a program needn't handle non-finite values.
Results may differ from a plain program's by a relative error of at most 0.0043.
Values may be sent and summed in bfloat16 or wider, within the bound.
No kernel may reach another device: no remote copies, remote signals or barrier semaphores. Data moves between devices by JAX's collectives and lax.ppermute only.
A program may use at most 64 MiB of HBM per device.

v0:
```python
import math

import jax
import jax.numpy as jnp
from jax import lax
from jax.sharding import PartitionSpec as P

VOX = 512


bias_first = 0.9999734386011124
bias_second = 0.095207852886291


def adam_step(param, grad, moment, second):
    new_moment = 0.9 * moment + 0.1 * grad
    new_second = 0.999 * second + 0.001 * grad * grad
    update = new_moment / bias_first / (jnp.sqrt(new_second / bias_second) + 1e-08)
    return (param - 0.05 * update, new_moment, new_second)


def body(
    latents,
    noise,
    timesteps,
    master_weight,
    norm_gain,
    weight_moment,
    weight_second,
    gain_moment,
    gain_second,
):
    rows, width = latents.shape
    shard_count = lax.axis_size("shard")
    replica_count = lax.axis_size("replica")
    total_rows = rows * shard_count * replica_count
    block_index = lax.axis_index("shard") * replica_count + lax.axis_index("replica")
    row_ids = block_index * rows + jnp.arange(rows, dtype=jnp.int32)
    step_time = timesteps[row_ids // VOX].astype(jnp.float32)
    level = jnp.cos((step_time / 1000.0 + 0.008) / 1.008 * (math.pi / 2)) ** 2
    noisy = jnp.sqrt(level)[:, None] * latents.astype(jnp.float32) + jnp.sqrt(1.0 - level)[
        :, None
    ] * noise.astype(jnp.float32)
    half = width // 2
    freqs = jnp.exp(-(2.0 * jnp.arange(half, dtype=jnp.float32) / width) * math.log(10000.0))
    angles = step_time[:, None] * freqs[None, :]
    embed = jnp.concatenate([jnp.sin(angles), jnp.cos(angles)], axis=1)
    mean = jnp.mean(noisy, axis=1, keepdims=True)
    var = jnp.mean((noisy - mean) ** 2, axis=1, keepdims=True)
    normed = (noisy - mean) / jnp.sqrt(var + 1e-05)
    full_gain = lax.all_gather(norm_gain, "shard", axis=0, tiled=True)
    hidden = normed * full_gain[None, :] + embed
    act = jax.nn.silu(hidden).astype(jnp.bfloat16)
    mixing_part = master_weight.astype(jnp.bfloat16)
    scale = 1.0 / math.sqrt(total_rows)
    columns = act
    product = jnp.dot(
        columns,
        lax.all_gather(mixing_part, "shard", axis=0, tiled=True),
        preferred_element_type=jnp.float32,
    )
    predicted = noisy + product
    grad_out = ((predicted - noise.astype(jnp.float32)) * scale).astype(jnp.bfloat16)
    grad_act = lax.dot_general(
        grad_out,
        lax.all_gather(mixing_part, "shard", axis=0, tiled=True),
        (((1,), (1,)), ((), ())),
        preferred_element_type=jnp.float32,
    )
    columns = act
    weight_share = lax.psum_scatter(
        lax.dot_general(
            columns, grad_out, (((0,), (0,)), ((), ())), preferred_element_type=jnp.float32
        ),
        "shard",
        scatter_dimension=0,
        tiled=True,
    )
    sig = jax.nn.sigmoid(hidden)
    grad_hidden = grad_act * (sig * (1.0 + hidden * (1.0 - sig)))
    gain_local = jnp.sum(grad_hidden * normed, axis=0)
    gain_share = lax.psum_scatter(gain_local, "shard", scatter_dimension=0, tiled=True)
    weight_grad, gain_grad = lax.psum((weight_share, gain_share), "replica")
    new_weight, new_wm, new_ws = adam_step(master_weight, weight_grad, weight_moment, weight_second)
    new_gain, new_gm, new_gs = adam_step(norm_gain, gain_grad, gain_moment, gain_second)
    return (new_weight, new_wm, new_ws, new_gain, new_gm, new_gs)


def solution(mesh):
    placed = (
        P(("shard", "replica"), None),
        P(("shard", "replica"), None),
        P(),
        P("shard", None),
        P("shard"),
        P("shard", None),
        P("shard", None),
        P("shard"),
        P("shard"),
    )
    return jax.shard_map(
        body,
        mesh=mesh,
        in_specs=placed,
        out_specs=(
            P("shard", None),
            P("shard", None),
            P("shard", None),
            P("shard"),
            P("shard"),
            P("shard"),
        ),
        check_vma=False,
    )
```

profile of v0, /device:TPU:0, one launch (start us, length us, event | category | flops | bytes accessed | tf_op | source)
XLA Modules:
  0.0 290.6 jit_solution(5563058571075944746)
XLA Ops:
  7.2 1.8 convert_element_type.33
  9.1 0.0 reduce-scatter.2.cloned.1.call-start
  9.1 1.3 fusion.13
  11.1 0.9 dynamic-update-slice
  12.2 44.2 %all-reduce = f32[1280]{0:T(1024)S(1)} all-reduce(f32[1280]{0:T(1024)S(1)} %dynamic-update-slice), channel_id=1, replica_groups=mesh['shard'=16,'replica'=2] {'shard'}, use_global_device_ids=true, to_apply=%add | all-reduce | flops 1280 | bytes 10240
  56.4 2.0 fusion.14
  58.3 4.3 %compare_select_fusion.1 = s32[256,1]{0,1:T(1,128)S(1)} fusion(s32[]{:T(128)} %bitcast.9, s32[]{:T(128)} %bitcast.10, s32[]{:T(128)} %bitcast.11, s32[]{:T(128)} %bitcast.12, s32[]{:T(128)} %bitcast.13, s32[]{:T(128)} %bitcast.15, s32[]{:T(128)} %bitcast.14, s32[]{:T(128)S(6)} %mul.160), kind=kLoop, calls=%fused_computation.32 | loop fusion | flops 7936 | bytes 1056 | tf_op jit(solution)/shard_map/gather | solution.py:39
  62.7 5.8 %fusion.9 = (f32[256]{0:T(256)S(1)}, f32[256]{0:T(256)S(1)}) fusion(pred[256]{0:T(512)(128)(4,1)S(1)} %get-tuple-element.34, pred[256]{0:T(512)(128)(4,1)S(1)} %get-tuple-element.35, pred[256]{0:T(512)(128)(4,1)S(1)} %get-tuple-element.36, pred[256]{0:T(512)(128)(4,1)S(1)} %get-tuple-element.37, pred[256]{0:T(512)(128)(4,1)S(1)} %get-tuple-element.38, ...), kind=kLoop, calls=%fused_computation.52 | loop fusion | flops 3584 | bytes 5412 | tf_op jit(solution)/shard_map/sqrt | solution.py:41
  68.5 0.1 subtract_sqrt_fusion
  68.6 1.5 fusion.6
  70.1 0.5 multiply_reduce_fusion
  70.6 2.4 multiply_sine_fusion
  73.0 10.6 %all-gather.2.cloned.1.call-done = bf16[1280,1280]{1,0:T(8,128)(2,1)} async-done(((bf16[80,1280]{1,0:T(8,128)(2,1)}), bf16[1280,1280]{1,0:T(8,128)(2,1)}) %all-gather.2.cloned.1.call-update) | async-done | bytes 3276816 | tf_op jit(solution)/shard_map/all_gather | solution.py:59
  83.5 3.5 %fusion.3 = bf16[256,1280]{1,0:T(8,128)(2,1)S(1)} fusion(bf16[1280,1280]{1,0:T(8,128)(2,1)} %all-gather.2.cloned.1.call-done, bf16[256,1280]{1,0:T(8,128)(2,1)S(1)} %copy-done, bf16[256,1280]{1,0:T(8,128)(2,1)S(1)} %copy-done.1, f32[256]{0:T(256)S(1)} %subtract_sqrt_fusion, f32[256]{0:T(256)S(1)} %get-tuple-element.12, ...), kind=kOutput, calls=%fused_computation.5 | convolution fusion | flops 846725120 | bytes 6562816 | tf_op jit(solution)/shard_map/dot_general | solution.py:57
  87.0 0.8 copy-done.7
  87.8 4.4 %fusion.10 = f32[1280,1280]{1,0:T(8,128)} fusion(bf16[256,1280]{1,0:T(8,128)(2,1)S(1)} %fusion.3, f32[256,640]{1,0:T(8,128)S(1)} %get-tuple-element.15, f32[256,640]{1,0:T(8,128)S(1)} %get-tuple-element.14, f32[1280]{0:T(1024)S(1)} %all-reduce, f32[256]{0:T(256)S(1)} %add_sqrt_fusion, f32[256]{0:T(256)S(1)} %broadcast_multiply_fusion, ...), kind=kOutput, calls=%fused_computation.53 | convolution fusion | flops 843776000 | bytes 9839616 | tf_op jit(solution)/shard_map/dot_general | solution.py:72
  92.3 0.0 all-reduce.4.cloned.1.call-start
  93.0 139.3 %reduce-scatter.2.cloned.1.call-done = f32[80,1280]{1,0:T(8,128)} async-done(((f32[1280,1280]{1,0:T(8,128)}), f32[80,1280]{1,0:T(8,128)}) %reduce-scatter.2.cloned.1.call-update) | async-done | bytes 409616 | tf_op jit(solution)/shard_map/reduce_scatter | solution.py:71
  232.4 3.6 %fusion.5 = f32[1280]{0:T(1024)S(1)} fusion(bf16[256,1280]{1,0:T(8,128)(2,1)} %copy-done.7, bf16[1280,1280]{1,0:T(8,128)(2,1)} %all-gather.2.cloned.1.call-done, f32[256,640]{1,0:T(8,128)S(1)} %get-tuple-element.15, f32[256,640]{1,0:T(8,128)S(1)} %get-tuple-element.14, f32[1280]{0:T(1024)S(1)} %all-reduce, f32[256]{0:T(256)S(1)} %add_sqrt_fusion, ...), kind=kOutput, calls=%fused_computation.13 | convolution fusion | flops 845413120 | bytes 6567936 | tf_op jit(solution)/shard_map/dot_general | solution.py:64
  236.0 42.7 %all-reduce.1 = f32[1280]{0:T(1024)S(1)} all-reduce(f32[1280]{0:T(1024)S(1)} %fusion.5), channel_id=3, replica_groups=mesh['shard'=16,'replica'=2] {'shard'}, use_global_device_ids=true, to_apply=%region_5.6.clone | all-reduce | flops 1280 | bytes 10240
  278.7 0.1 dynamic-slice.2
  278.8 2.4 psum.15
  281.2 0.5 multiply_subtract_fusion.1
  281.8 2.3 multiply_subtract_fusion
  (29 shorter events, 0.3 us)
Async XLA Ops:
  7.2 61.4 %copy-start = (bf16[256,1280]{1,0:T(8,128)(2,1)S(1)}, bf16[256,1280]{1,0:T(8,128)(2,1)}, u32[]{:S(2)}) copy-start(bf16[256,1280]{1,0:T(8,128)(2,1)} %param.10) | copy-start | bytes 1966084
  7.2 62.9 %copy-start.1 = (bf16[256,1280]{1,0:T(8,128)(2,1)S(1)}, bf16[256,1280]{1,0:T(8,128)(2,1)}, u32[]{:S(2)}) copy-start(bf16[256,1280]{1,0:T(8,128)(2,1)} %param.9) | copy-start | bytes 1966084
  7.2 76.4 %all-gather.2.cloned.1.call-start = ((), (), s32[]{:S(2)}) async-start(), calls=%async_computation.1 | async-start | bytes 3481600 | tf_op jit(solution)/shard_map/all_gather | solution.py:59
  9.1 223.3 %reduce-scatter.2.cloned.1.call-start = ((), (), s32[]{:S(2)}) async-start(), calls=%async_computation.2 | async-start | bytes 6963200 | tf_op jit(solution)/shard_map/reduce_scatter | solution.py:71
  87.0 0.8 copy-start.7
  92.3 189.5 %all-reduce.4.cloned.1.call-start = ((), (), s32[]{:S(2)}) async-start(), calls=%async_computation.3 | async-start | bytes 819200 | tf_op jit(solution)/shard_map/psum | solution.py:83
  232.3 48.9 %copy-start.4 = (f32[80]{0:T(128)S(1)}, f32[80]{0:T(128)}, u32[]{:S(2)}) copy-start(f32[80]{0:T(128)} %param.13) | copy-start | bytes 964
  232.4 48.9 %copy-start.5 = (f32[80]{0:T(128)S(1)}, f32[80]{0:T(128)}, u32[]{:S(2)}) copy-start(f32[80]{0:T(128)} %param.16) | copy-start | bytes 964
  232.4 48.9 %copy-start.6 = (f32[80]{0:T(128)S(1)}, f32[80]{0:T(128)}, u32[]{:S(2)}) copy-start(f32[80]{0:T(128)} %param.17) | copy-start | bytes 964
  232.4 49.4 %copy-start.2 = (f32[80,1280]{1,0:T(8,128)S(1)}, f32[80,1280]{1,0:T(8,128)}, u32[]{:S(2)}) copy-start(f32[80,1280]{1,0:T(8,128)} %param.12) | copy-start | bytes 1228804
  232.4 49.4 %copy-start.3 = (f32[80,1280]{1,0:T(8,128)S(1)}, f32[80,1280]{1,0:T(8,128)}, u32[]{:S(2)}) copy-start(f32[80,1280]{1,0:T(8,128)} %param.14) | copy-start | bytes 1228804
Sparse Core Ops, SparseCore 0:
  11.3 72.1 all-gather.1
  92.4 139.8 reduce-scatter.1
  234.8 20.4 all-reduce.3
where the time goes:
time: 291 us
  waiting for transfers between devices  150 us (52%)
  blocking collectives  89.3 us (31%)
  other arithmetic  19.4 us (7%)
  between operations  15.2 us (5%)
  matrix products  11.5 us (4%)
  local copies, waits for them, and re-layouts  5.13 us (2%)
    reduce_scatter x1, waiting for transfers between devices, body(): lax.psum_scatter(lax.dot_general(columns, grad_out, (((0,), (0,)), ((), (...  139 us
    unnamed x2, blocking collectives  86.9 us
    all_gather x1, waiting for transfers between devices, body(): lax.all_gather(mixing_part, 'shard', axis=0, tiled=True)  10.6 us
  transfers between devices with their start and end apart: 3, of which 2 were waited for; matrix products, arithmetic and copies ran while one was open for 8% of the time, Pallas kernels for 0%

commit v1 on v0

v1 whole, which is shorter than its diff:
```python
import functools
import math

import jax
import jax.numpy as jnp
from jax import lax
from jax.experimental import pallas as pl
from jax.experimental.pallas import tpu as pltpu
from jax.sharding import PartitionSpec as P

VOX = 512
AXES = ("shard", "replica")
BF = jnp.bfloat16
F32 = jnp.float32

bias_first = 0.9999734386011124
bias_second = 0.095207852886291


def adam_step(param, grad, moment, second):
    new_moment = 0.9 * moment + 0.1 * grad
    new_second = 0.999 * second + 0.001 * grad * grad
    update = new_moment / bias_first / (jnp.sqrt(new_second / bias_second) + 1e-08)
    return (param - 0.05 * update, new_moment, new_second)


def frequencies(width):
    half = width // 2
    return jnp.exp(-(2.0 * jnp.arange(half, dtype=F32) / width) * math.log(10000.0))


def noise_level(step_time):
    return jnp.cos((step_time / 1000.0 + 0.008) / 1.008 * (math.pi / 2)) ** 2


def general_body(
    latents, noise, timesteps, master_weight, norm_gain, weight_moment, weight_second, gain_moment, gain_second
):
    rows, width = latents.shape
    shard_count = lax.axis_size("shard")
    replica_count = lax.axis_size("replica")
    total_rows = rows * shard_count * replica_count
    block_index = lax.axis_index("shard") * replica_count + lax.axis_index("replica")
    row_ids = block_index * rows + jnp.arange(rows, dtype=jnp.int32)
    step_time = timesteps[row_ids // VOX].astype(F32)
    level = noise_level(step_time)
    noisy = (
        jnp.sqrt(level)[:, None] * latents.astype(F32)
        + jnp.sqrt(1.0 - level)[:, None] * noise.astype(F32)
    )
    angles = step_time[:, None] * frequencies(width)[None, :]
    embed = jnp.concatenate([jnp.sin(angles), jnp.cos(angles)], axis=1)
    mean = jnp.mean(noisy, axis=1, keepdims=True)
    var = jnp.mean((noisy - mean) ** 2, axis=1, keepdims=True)
    normed = (noisy - mean) / jnp.sqrt(var + 1e-05)
    full_gain = lax.all_gather(norm_gain, "shard", axis=0, tiled=True)
    hidden = normed * full_gain[None, :] + embed
    act = jax.nn.silu(hidden).astype(BF)
    mixing = lax.all_gather(master_weight.astype(BF), "shard", axis=0, tiled=True)
    scale = 1.0 / math.sqrt(total_rows)
    predicted = noisy + jnp.dot(act, mixing, preferred_element_type=F32)
    grad_out = ((predicted - noise.astype(F32)) * scale).astype(BF)
    grad_act = lax.dot_general(
        grad_out, mixing, (((1,), (1,)), ((), ())), preferred_element_type=F32
    )
    weight_share = lax.psum_scatter(
        lax.dot_general(act, grad_out, (((0,), (0,)), ((), ())), preferred_element_type=F32),
        "shard",
        scatter_dimension=0,
        tiled=True,
    )
    sig = jax.nn.sigmoid(hidden)
    grad_hidden = grad_act * (sig * (1.0 + hidden * (1.0 - sig)))
    gain_local = jnp.sum(grad_hidden * normed, axis=0)
    gain_share = lax.psum_scatter(gain_local, "shard", scatter_dimension=0, tiled=True)
    weight_grad, gain_grad = lax.psum((weight_share, gain_share), "replica")
    return (
        *adam_step(master_weight, weight_grad, weight_moment, weight_second),
        *adam_step(norm_gain, gain_grad, gain_moment, gain_second),
    )


VMEM = pl.BlockSpec(memory_space=pltpu.VMEM)
SMEM = pl.BlockSpec(memory_space=pltpu.SMEM)


def act_kernel(half, pos_ref, coef_ref, gain_ref, embed_ref, l0, n0, l1, n1, act_ref, slope_ref, diff_ref):
    width = act_ref.shape[1]
    col = pl.ds(pl.multiple_of(pos_ref[1] * half, 128), half)
    a, b = coef_ref[0], coef_ref[1]
    gain = gain_ref[...]
    embed = embed_ref[...]
    tile = 16
    for part, (l_ref, n_ref) in enumerate(((l0, n0), (l1, n1))):
        rows = l_ref.shape[0]

        def step(i, carry, l_ref=l_ref, n_ref=n_ref, base=part * rows):
            at = pl.ds(pl.multiple_of(i * tile, tile), tile)
            to = pl.ds(pl.multiple_of(base + i * tile, tile), tile)
            noisy = a * l_ref[at, :].astype(F32) + b * n_ref[at, :].astype(F32)
            mean = jnp.sum(noisy, axis=1, keepdims=True) * (1.0 / width)
            cent = noisy - mean
            var = jnp.sum(cent * cent, axis=1, keepdims=True) * (1.0 / width)
            normed = cent * (1.0 / jnp.sqrt(var + 1e-05))
            hidden = normed * gain + embed
            sig = 1.0 / (1.0 + jnp.exp(-hidden))
            act_ref[to, :] = (hidden * sig).astype(BF)
            slope_ref[to, :] = sig * (1.0 + hidden * (1.0 - sig)) * normed
            nh = n_ref[at, col].astype(F32)
            diff_ref[to, :] = (a * l_ref[at, col].astype(F32) + b * nh) - nh
            return carry

        lax.fori_loop(0, rows // tile, step, 0)


def mix_kernel(
    scale, unit, pos_ref, act_ref, diff_ref, wa, wa1, wa2, wb, wb1, wb2,
    gout_ref, w_ref, send_a, send_b, keep_a, keep_b, wg_ref,
):
    me = pos_ref[0]

    def place(kz, kp):
        return pl.ds(pl.multiple_of((me ^ (kz * 4 + kp)) * unit, 16), unit)

    def rows(i):
        return pl.ds(i * unit, unit)

    for k in range(2):
        w_ref[place(k, 0), :] = wa[rows(k), :]
        w_ref[place(k, 1), :] = wa1[rows(k), :]
        w_ref[place(k, 2), :] = wa2[rows(k), :]
        w_ref[place(k, 3), :] = wa2[rows(2 + k), :]
        w_ref[place(2 + k, 0), :] = wb[rows(k), :]
        w_ref[place(2 + k, 2), :] = wb1[rows(k), :]
        w_ref[place(2 + k, 1), :] = wb2[rows(k), :]
        w_ref[place(2 + k, 3), :] = wb2[rows(2 + k), :]
    product = jnp.dot(act_ref[...], w_ref[...], preferred_element_type=F32)
    gout_ref[...] = ((diff_ref[...] + product) * scale).astype(BF)
    wg_ref[...] = lax.dot_general(
        act_ref[...], gout_ref[...], (((0,), (0,)), ((), ())), preferred_element_type=F32
    )
    for k in range(2):
        send_a[rows(k), :] = wg_ref[place(k, 1), :].astype(BF)
        send_a[rows(2 + k), :] = wg_ref[place(k, 3), :].astype(BF)
        keep_a[rows(k), :] = wg_ref[place(k, 0), :]
        keep_a[rows(2 + k), :] = wg_ref[place(k, 2), :]
        send_b[rows(k), :] = wg_ref[place(2 + k, 2), :].astype(BF)
        send_b[rows(2 + k), :] = wg_ref[place(2 + k, 3), :].astype(BF)
        keep_b[rows(k), :] = wg_ref[place(2 + k, 0), :]
        keep_b[rows(2 + k), :] = wg_ref[place(2 + k, 1), :]


def gain_kernel(gout_ref, w_ref, slope_ref, out_ref):
    grad_act = lax.dot_general(
        gout_ref[...], w_ref[...], (((1,), (1,)), ((), ())), preferred_element_type=F32
    )
    out_ref[...] = jnp.sum(grad_act * slope_ref[...], axis=0, keepdims=True)


def paired_body(
    latents, noise, timesteps, master_weight, norm_gain, weight_moment, weight_second, gain_moment, gain_second
):
    rows, width = latents.shape
    unit = master_weight.shape[0]
    shards, cores = lax.axis_size("shard"), lax.axis_size("replica")
    total_rows = rows * shards * cores
    half = width // 2
    me, core = lax.axis_index("shard"), lax.axis_index("replica")
    pos = jnp.stack([me, core]).astype(jnp.int32)

    def to(x, k):
        pairs = [(i * cores + c, (i ^ k) * cores + c) for i in range(shards) for c in range(cores)]
        return lax.ppermute(x, AXES, pairs)

    def across(x):
        pairs = [(i * cores + c, i * cores + 1 - c) for i in range(shards) for c in range(cores)]
        return lax.ppermute(x, AXES, pairs)

    def call(kernel, outs, specs, scratch=(), flops=0, byts=0):
        return pl.pallas_call(
            kernel,
            out_shape=outs,
            in_specs=specs,
            out_specs=jax.tree.map(lambda _: VMEM, outs),
            scratch_shapes=list(scratch),
            compiler_params=pltpu.CompilerParams(vmem_limit_bytes=40 << 20),
            cost_estimate=pl.CostEstimate(flops=flops, bytes_accessed=byts, transcendentals=0),
        )

    arr = jax.ShapeDtypeStruct

    own = lax.dynamic_slice(master_weight, (0, core * half), (unit, half)).astype(BF)
    z1, z2, z3 = to(own, 4), to(own, 8), to(own, 12)
    wa = jnp.concatenate([own, z1], axis=0)
    wa1 = to(wa, 1)
    wb = jnp.concatenate([z2, z3], axis=0)
    wb1 = to(wb, 2)
    wa2 = to(jnp.concatenate([wa, wa1], axis=0), 2)
    wb2 = to(jnp.concatenate([wb, wb1], axis=0), 1)

    gain = lax.dynamic_update_slice(
        jnp.zeros((1, width), F32), norm_gain.reshape(1, unit), (0, me * unit)
    )
    gain = gain + to(gain, 4) + to(gain, 8) + to(gain, 12)
    gain = gain + to(gain, 1)
    gain = gain + to(gain, 2)

    other_latents, other_noise = across(latents), across(noise)
    step_time = lax.dynamic_slice(timesteps, (me * cores * rows // VOX,), (1,)).astype(F32)
    level = noise_level(step_time)
    coef = jnp.concatenate([jnp.sqrt(level), jnp.sqrt(1.0 - level)])
    angles = step_time[:, None] * frequencies(width)[None, :]
    embed = jnp.concatenate([jnp.sin(angles), jnp.cos(angles)], axis=1)
    both = rows * cores
    act, slope, diff = call(
        functools.partial(act_kernel, half),
        (arr((both, width), BF), arr((both, width), F32), arr((both, half), F32)),
        [SMEM, SMEM] + [VMEM] * 6,
        flops=30 * both * width,
        byts=8 * both * width,
    )(pos, coef, gain, embed, latents, noise, other_latents, other_noise)

    gout, mixing, send_a, send_b, keep_a, keep_b = call(
        functools.partial(mix_kernel, 1.0 / math.sqrt(total_rows), unit),
        (
            arr((both, half), BF),
            arr((width, half), BF),
            arr((4 * unit, half), BF),
            arr((4 * unit, half), BF),
            arr((4 * unit, half), F32),
            arr((4 * unit, half), F32),
        ),
        [SMEM] + [VMEM] * 8,
        [pltpu.VMEM((width, half), F32)],
        flops=4 * both * width * half,
        byts=6 * both * width,
    )(pos, act, diff, wa, wa1, wa2, wb, wb1, wb2)

    got_a, got_b = to(send_a, 1), to(send_b, 2)
    part = call(
        gain_kernel,
        arr((1, width), F32),
        [VMEM] * 3,
        flops=2 * both * width * half,
        byts=6 * both * width,
    )(gout, mixing, slope)

    two, one = 2 * unit, unit
    sum_a = keep_a + got_a.astype(F32)
    sum_b = keep_b + got_b.astype(F32)
    got_a2 = to(sum_a[two:].astype(BF), 2)
    got_b2 = to(sum_b[two:].astype(BF), 1)
    sum_a = sum_a[:two] + got_a2.astype(F32)
    sum_b = sum_b[:two] + got_b2.astype(F32)
    h1 = to(sum_a[one:].astype(BF), 4)
    h2 = to(sum_b[:one].astype(BF), 8)
    h3 = to(sum_b[one:].astype(BF), 12)
    mine = sum_a[:one] + h1.astype(F32) + h2.astype(F32) + h3.astype(F32)

    for k in (1, 2, 4, 8):
        part = part + to(part, k)
    part = part + across(part)
    gain_grad = lax.dynamic_slice(part, (0, me * unit), (1, unit)).reshape(unit)

    theirs = across(mine)
    weight_grad = jnp.where(
        core == 0,
        jnp.concatenate([mine, theirs], axis=1),
        jnp.concatenate([theirs, mine], axis=1),
    )
    return (
        *adam_step(master_weight, weight_grad, weight_moment, weight_second),
        *adam_step(norm_gain, gain_grad, gain_moment, gain_second),
    )


def body(latents, *rest):
    rows, width = latents.shape
    unit = rest[2].shape[0]
    paired = (
        lax.axis_size("shard") == 16
        and lax.axis_size("replica") == 2
        and unit % 16 == 0
        and width % 256 == 0
        and rows % 16 == 0
        and VOX % (2 * rows) == 0
    )
    return (paired_body if paired else general_body)(latents, *rest)


def solution(mesh):
    rows = P(AXES, None)
    block = P("shard", None)
    line = P("shard")
    return jax.shard_map(
        body,
        mesh=mesh,
        in_specs=(rows, rows, P(), block, line, block, block, line, line),
        out_specs=(block, block, block, line, line, line),
        check_vma=False,
    )
```

time: 291 us -> 100 us (0.34)
  waiting for transfers between devices: 150 us -> 47.2 us
  blocking collectives: 89.3 us -> 0 us
  starting transfers between devices: 0.12 us -> 32 us
  other arithmetic: 19.4 us -> 3.28 us
  between operations: 15.2 us -> 1.79 us
  Pallas kernels: 0 us -> 12.7 us
  matrix products: 11.5 us -> 0 us
    reduce_scatter x1 -> x0, waiting for transfers between devices: 139 us -> none  [body(): lax.psum_scatter(lax.dot_general(columns, grad_out, (((0,), (0,)), ((), (...]
    unnamed x2 -> x0, blocking collectives: 86.9 us -> none
    ppermute x0 -> x27, waiting for transfers between devices: none -> 47.2 us  [the longest x23 46.7 us: to(): return lax.ppermute(x, AXES, pairs)]
    ppermute x0 -> x27, starting transfers between devices: none -> 32 us  [the longest x23 31.3 us: to(): return lax.ppermute(x, AXES, pairs)]
    pallas_call x0 -> x3, Pallas kernels: none -> 12.7 us  [the longest x1 8.34 us: paired_body(): call(functools.partial(act_kernel, half), (arr((both, width), BF), arr((b...]
    dot_general x3 -> x0, matrix products: 11.5 us -> none  [the longest x1 4.42 us: body(): lax.dot_general(columns, grad_out, (((0,), (0,)), ((), ())), preferred_el...]
    all_gather x1 -> x0, waiting for transfers between devices: 10.6 us -> none  [body(): lax.all_gather(mixing_part, 'shard', axis=0, tiled=True)]
    sqrt x3 -> x0, other arithmetic: 5.88 us -> none  [the longest x1 5.82 us: body(): jnp.sqrt(level)[:, None] * latents.astype(jnp.float32)]
  transfers between devices with their start and end apart: 3 -> 27, of which waited for: 2 -> 14; matrix products, arithmetic and copies ran while one was open for 8% -> 4% of each run, Pallas kernels for 0% -> 10%
where the time goes in v1:
time: 100 us
  waiting for transfers between devices  47.2 us (47%)
  starting transfers between devices  32 us (32%)
  Pallas kernels  12.7 us (13%)
  other arithmetic  3.28 us (3%)
  local copies, waits for them, and re-layouts  3.24 us (3%)
  between operations  1.79 us (2%)
    ppermute x23, waiting for transfers between devices, to(): return lax.ppermute(x, AXES, pairs)  46.7 us
    ppermute x23, starting transfers between devices, to(): return lax.ppermute(x, AXES, pairs)  31.3 us
    pallas_call x1, Pallas kernels, paired_body(): call(functools.partial(act_kernel, half), (arr((both, width), BF), arr((b...  8.34 us
    pallas_call x1, Pallas kernels, paired_body(): call(functools.partial(mix_kernel, 1.0 / math.sqrt(total_rows), unit), (a...  3.11 us
  transfers between devices with their start and end apart: 27, of which 14 were waited for; matrix products, arithmetic and copies ran while one was open for 4% of the time, Pallas kernels for 10%

profile of v1, /device:TPU:0, one launch (start us, length us, event | category | flops | bytes accessed | tf_op | source)
XLA Modules:
  0.0 100.2 jit_solution(16273454402899066418)
XLA Ops:
  1.5 5.2 %collective-permute-start.2 = (f32[1,1280]{1,0:T(1,128)S(1)}, f32[1,1280]{1,0:T(1,128)S(1)}, u32[]{:S(2)}, u32[]{:S(2)}) collective-permute-start(f32[1,1280]{1,0:T(1,128)S(1)} %dynamic_update_slice.5), channel_id=1, source_target_pairs={{0,24},{1,25},{2,26},{3,27},{4,28},{5,29},{6,30},{7,31},{8,16},{9,... | collective-permute-start | bytes 15368 | tf_op jit(solution)/shard_map/ppermute | solution.py:173
  8.3 3.8 %collective-permute-start.11 = (bf16[80,640]{1,0:T(8,128)(2,1)S(1)}, bf16[80,640]{1,0:T(8,128)(2,1)S(1)}, u32[]{:S(2)}, u32[]{:S(2)}) collective-permute-start(bf16[80,640]{1,0:T(8,128)(2,1)S(1)} %dynamic-slice_convert_fusion), channel_id=1, source_target_pairs={{0,24},{1,25},{2,26},{3,27},{4,28},{5,29},{6,30},{7,31},{8,16},{9,... | collective-permute-start | bytes 307208 | tf_op jit(solution)/shard_map/ppermute | solution.py:173
  14.2 5.8 %collective-permute-done.10 = bf16[80,640]{1,0:T(8,128)(2,1)S(1)} collective-permute-done((bf16[80,640]{1,0:T(8,128)(2,1)S(1)}, bf16[80,640]{1,0:T(8,128)(2,1)S(1)}, u32[]{:S(2)}, u32[]{:S(2)}) %collective-permute-start.10) | collective-permute-done | bytes 102432 | tf_op jit(solution)/shard_map/ppermute | solution.py:173
  20.1 4.5 %collective-permute-done.7 = bf16[80,640]{1,0:T(8,128)(2,1)S(1)} collective-permute-done((bf16[80,640]{1,0:T(8,128)(2,1)S(1)}, bf16[80,640]{1,0:T(8,128)(2,1)S(1)}, u32[]{:S(2)}, u32[]{:S(2)}) %collective-permute-start.7) | collective-permute-done | bytes 102432 | tf_op jit(solution)/shard_map/ppermute | solution.py:173
  26.1 1.5 %collective-permute-start.8 = (bf16[160,640]{1,0:T(8,128)(2,1)S(1)}, bf16[160,640]{1,0:T(8,128)(2,1)S(1)}, u32[]{:S(2)}, u32[]{:S(2)}) collective-permute-start(bf16[160,640]{1,0:T(8,128)(2,1)S(1)} %pad_maximum_fusion.2.wa), channel_id=1, source_target_pairs={{0,2},{1,3},{2,0},{3,1},{4,6},{5,7},{6,4},{7,5},{8,10},{9,11},{10,... | collective-permute-start | bytes 614408 | tf_op jit(solution)/shard_map/ppermute | solution.py:173
  28.5 3.5 %collective-permute-done.8.wa1 = bf16[160,640]{1,0:T(8,128)(2,1)S(1)} collective-permute-done((bf16[160,640]{1,0:T(8,128)(2,1)S(1)}, bf16[160,640]{1,0:T(8,128)(2,1)S(1)}, u32[]{:S(2)}, u32[]{:S(2)}) %collective-permute-start.8) | collective-permute-done | bytes 204832 | tf_op jit(solution)/shard_map/ppermute | solution.py:173
  32.6 1.6 %collective-permute-start.13 = (bf16[320,640]{1,0:T(8,128)(2,1)S(1)}, bf16[320,640]{1,0:T(8,128)(2,1)S(1)}, u32[]{:S(2)}, u32[]{:S(2)}) collective-permute-start(bf16[320,640]{1,0:T(8,128)(2,1)S(1)} %pad_maximum_fusion.1), channel_id=1, source_target_pairs={{0,2},{1,3},{2,0},{3,1},{4,6},{5,7},{6,4},{7,5},{8,10},{9,11},{10,... | collective-permute-start | bytes 1228808 | tf_op jit(solution)/shard_map/ppermute | solution.py:173
  35.1 9.4 %collective-permute-done.3 = f32[1,1280]{1,0:T(1,128)S(1)} collective-permute-done((f32[1,1280]{1,0:T(1,128)S(1)}, f32[1,1280]{1,0:T(1,128)S(1)}, u32[]{:S(2)}, u32[]{:S(2)}) %collective-permute-start.3) | collective-permute-done | bytes 5152 | tf_op jit(solution)/shard_map/ppermute | solution.py:173
  44.4 1.6 %collective-permute-start.4 = (f32[1,1280]{1,0:T(1,128)S(1)}, f32[1,1280]{1,0:T(1,128)S(1)}, u32[]{:S(2)}, u32[]{:S(2)}) collective-permute-start(f32[1,1280]{1,0:T(1,128)S(1)} %add.96), channel_id=1, source_target_pairs={{0,4},{1,5},{2,6},{3,7},{4,0},{5,1},{6,2},{7,3},{8,12},{9,13},{10,... | collective-permute-start | bytes 15368 | tf_op jit(solution)/shard_map/ppermute | solution.py:173
  46.1 2.0 %collective-permute-done.4 = f32[1,1280]{1,0:T(1,128)S(1)} collective-permute-done((f32[1,1280]{1,0:T(1,128)S(1)}, f32[1,1280]{1,0:T(1,128)S(1)}, u32[]{:S(2)}, u32[]{:S(2)}) %collective-permute-start.4) | collective-permute-done | bytes 5152 | tf_op jit(solution)/shard_map/ppermute | solution.py:173
  48.1 8.3 %shard_map.136 = (bf16[512,1280]{1,0:T(8,128)(2,1)S(1)}, f32[512,1280]{1,0:T(8,128)S(1)}, f32[512,640]{1,0:T(8,128)S(1)}) custom-call(s32[2]{0:T(128)S(1)} %pad_add_fusion.pos_ref, f32[2]{0:T(128)S(1)} %pad_maximum_fusion.4.coef_ref, f32[1,1280]{1,0:T(1,128)S(1)} %add.97.gain_ref, f32[1,1280]{1,0:T(1,128)S(1)} %pad_maximum_fusion.3.embed_ref, ...), custom_call_target="tpu_custom_call" | custom-call | flops 19660800 | bytes 5242880 | tf_op jit(solution)/shard_map/pallas_call | solution.py:215
  56.5 3.1 %shard_map.137 = (bf16[512,640]{1,0:T(8,128)(2,1)S(1)}, bf16[1280,640]{1,0:T(8,128)(2,1)S(1)}, bf16[320,640]{1,0:T(8,128)(2,1)S(1)}, bf16[320,640]{1,0:T(8,128)(...) custom-call(s32[2]{0:T(128)S(1)} %pad_add_fusion.pos_ref, bf16[512,1280]{1,0:T(8,128)(2,1)S(1)} %get-tuple-element.15.act_ref, ...), custom_call_target="tpu_custom_call" | custom-call | flops 1677721600 | bytes 3932160 | tf_op jit(solution)/shard_map/pallas_call | solution.py:223
  59.6 1.6 %collective-permute-start.14 = (bf16[320,640]{1,0:T(8,128)(2,1)S(1)}, bf16[320,640]{1,0:T(8,128)(2,1)S(1)}, u32[]{:S(2)}, u32[]{:S(2)}) collective-permute-start(bf16[320,640]{1,0:T(8,128)(2,1)S(1)} %get-tuple-element.18), channel_id=1, source_target_pairs={{0,2},{1,3},{2,0},{3,1},{4,6},{5,7},{6,4},{7,5},{8,10},{9,11},{10,... | collective-permute-start | bytes 1228808 | tf_op jit(solution)/shard_map/ppermute | solution.py:173
  62.7 6.6 %collective-permute-done.14 = bf16[320,640]{1,0:T(8,128)(2,1)S(1)} collective-permute-done((bf16[320,640]{1,0:T(8,128)(2,1)S(1)}, bf16[320,640]{1,0:T(8,128)(2,1)S(1)}, u32[]{:S(2)}, u32[]{:S(2)}) %collective-permute-start.14) | collective-permute-done | bytes 409632 | tf_op jit(solution)/shard_map/ppermute | solution.py:173
  69.5 1.6 %collective-permute-start.15 = (bf16[160,640]{1,0:T(8,128)(2,1)S(1)}, bf16[160,640]{1,0:T(8,128)(2,1)S(1)}, u32[]{:S(2)}, u32[]{:S(2)}) collective-permute-start(bf16[160,640]{1,0:T(8,128)(2,1)S(1)} %slice.58), channel_id=1, source_target_pairs={{0,4},{1,5},{2,6},{3,7},{4,0},{5,1},{6,2},{7,3},{8,12},{9,13},{10,... | collective-permute-start | bytes 614408 | tf_op jit(solution)/shard_map/ppermute | solution.py:173
  72.7 2.6 %collective-permute-done.15 = bf16[160,640]{1,0:T(8,128)(2,1)S(1)} collective-permute-done((bf16[160,640]{1,0:T(8,128)(2,1)S(1)}, bf16[160,640]{1,0:T(8,128)(2,1)S(1)}, u32[]{:S(2)}, u32[]{:S(2)}) %collective-permute-start.15) | collective-permute-done | bytes 204832 | tf_op jit(solution)/shard_map/ppermute | solution.py:173
  75.4 2.1 %collective-permute-done.18 = bf16[160,640]{1,0:T(8,128)(2,1)S(1)} collective-permute-done((bf16[160,640]{1,0:T(8,128)(2,1)S(1)}, bf16[160,640]{1,0:T(8,128)(2,1)S(1)}, u32[]{:S(2)}, u32[]{:S(2)}) %collective-permute-start.18) | collective-permute-done | bytes 204832 | tf_op jit(solution)/shard_map/ppermute | solution.py:173
  78.6 1.5 %collective-permute-start.20 = (bf16[80,640]{1,0:T(8,128)(2,1)S(1)}, bf16[80,640]{1,0:T(8,128)(2,1)S(1)}, u32[]{:S(2)}, u32[]{:S(2)}) collective-permute-start(bf16[80,640]{1,0:T(8,128)(2,1)S(1)} %get-tuple-element.31), channel_id=1, source_target_pairs={{0,24},{1,25},{2,26},{3,27},{4,28},{5,29},{6,30},{7,31},{8,16},{9,... | collective-permute-start | bytes 307208 | tf_op jit(solution)/shard_map/ppermute | solution.py:173
  82.8 2.4 %collective-permute-done.22 = f32[1,1280]{1,0:T(1,128)S(1)} collective-permute-done((f32[1,1280]{1,0:T(1,128)S(1)}, f32[1,1280]{1,0:T(1,128)S(1)}, u32[]{:S(2)}, u32[]{:S(2)}) %collective-permute-start.22) | collective-permute-done | bytes 5152 | tf_op jit(solution)/shard_map/ppermute | solution.py:173
  85.2 1.5 %collective-permute-start.23 = (f32[1,1280]{1,0:T(1,128)S(1)}, f32[1,1280]{1,0:T(1,128)S(1)}, u32[]{:S(2)}, u32[]{:S(2)}) collective-permute-start(f32[1,1280]{1,0:T(1,128)S(1)} %add.110), channel_id=1, source_target_pairs={{0,4},{1,5},{2,6},{3,7},{4,0},{5,1},{6,2},{7,3},{8,12},{9,13},{10,... | collective-permute-start | bytes 15368 | tf_op jit(solution)/shard_map/ppermute | solution.py:173
  86.7 2.1 %collective-permute-done.23 = f32[1,1280]{1,0:T(1,128)S(1)} collective-permute-done((f32[1,1280]{1,0:T(1,128)S(1)}, f32[1,1280]{1,0:T(1,128)S(1)}, u32[]{:S(2)}, u32[]{:S(2)}) %collective-permute-start.23) | collective-permute-done | bytes 5152 | tf_op jit(solution)/shard_map/ppermute | solution.py:173
  89.9 2.7 %collective-permute-done.24 = f32[1,1280]{1,0:T(1,128)S(1)} collective-permute-done((f32[1,1280]{1,0:T(1,128)S(1)}, f32[1,1280]{1,0:T(1,128)S(1)}, u32[]{:S(2)}, u32[]{:S(2)}) %collective-permute-start.24) | collective-permute-done | bytes 5152 | tf_op jit(solution)/shard_map/ppermute | solution.py:173
  92.6 2.0 %collective-permute-start.25 = (f32[1,1280]{1,0:T(1,128)S(1)}, f32[1,1280]{1,0:T(1,128)S(1)}, u32[]{:S(2)}, u32[]{:S(2)}) collective-permute-start(f32[1,1280]{1,0:T(1,128)S(1)} %add.112), channel_id=1, source_target_pairs={{0,16},{1,17},{2,18},{3,19},{4,20},{5,21},{6,22},{7,23},{8,24},{9,... | collective-permute-start | bytes 15368 | tf_op jit(solution)/shard_map/ppermute | solution.py:173
  94.6 2.6 %collective-permute-done.25 = f32[1,1280]{1,0:T(1,128)S(1)} collective-permute-done((f32[1,1280]{1,0:T(1,128)S(1)}, f32[1,1280]{1,0:T(1,128)S(1)}, u32[]{:S(2)}, u32[]{:S(2)}) %collective-permute-start.25) | collective-permute-done | bytes 5152 | tf_op jit(solution)/shard_map/ppermute | solution.py:173
  (82 shorter events, 18.9 us)
Async XLA Ops:
  1.5 31.1 %collective-permute-start.2 = (f32[1,1280]{1,0:T(1,128)S(1)}, f32[1,1280]{1,0:T(1,128)S(1)}, u32[]{:S(2)}, u32[]{:S(2)}) collective-permute-start(f32[1,1280]{1,0:T(1,128)S(1)} %dynamic_update_slice.5), channel_id=1, source_target_pairs={{0,24},{1,25},{2,26},{3,27},{4,28},{5,29},{6,30},{7,31},{8,16},{9,... | collective-permute-start | bytes 15368 | tf_op jit(solution)/shard_map/ppermute | solution.py:173
  6.7 27.5 %collective-permute-start.1 = (f32[1,1280]{1,0:T(1,128)S(1)}, f32[1,1280]{1,0:T(1,128)S(1)}, u32[]{:S(2)}, u32[]{:S(2)}) collective-permute-start(f32[1,1280]{1,0:T(1,128)S(1)} %dynamic_update_slice.5), channel_id=1, source_target_pairs={{0,16},{1,17},{2,18},{3,19},{4,20},{5,21},{6,22},{7,23},{8,24},{9,... | collective-permute-start | bytes 15368 | tf_op jit(solution)/shard_map/ppermute | solution.py:173
  6.8 19.4 %collective-permute-start = (f32[1,1280]{1,0:T(1,128)S(1)}, f32[1,1280]{1,0:T(1,128)S(1)}, u32[]{:S(2)}, u32[]{:S(2)}) collective-permute-start(f32[1,1280]{1,0:T(1,128)S(1)} %dynamic_update_slice.5), channel_id=1, source_target_pairs={{0,8},{1,9},{2,10},{3,11},{4,12},{5,13},{6,14},{7,15},{8,0},{9,1},... | collective-permute-start | bytes 15368 | tf_op jit(solution)/shard_map/ppermute | solution.py:173
  8.3 11.6 %collective-permute-start.11 = (bf16[80,640]{1,0:T(8,128)(2,1)S(1)}, bf16[80,640]{1,0:T(8,128)(2,1)S(1)}, u32[]{:S(2)}, u32[]{:S(2)}) collective-permute-start(bf16[80,640]{1,0:T(8,128)(2,1)S(1)} %dynamic-slice_convert_fusion), channel_id=1, source_target_pairs={{0,24},{1,25},{2,26},{3,27},{4,28},{5,29},{6,30},{7,31},{8,16},{9,... | collective-permute-start | bytes 307208 | tf_op jit(solution)/shard_map/ppermute | solution.py:173
  12.1 7.8 %collective-permute-start.10 = (bf16[80,640]{1,0:T(8,128)(2,1)S(1)}, bf16[80,640]{1,0:T(8,128)(2,1)S(1)}, u32[]{:S(2)}, u32[]{:S(2)}) collective-permute-start(bf16[80,640]{1,0:T(8,128)(2,1)S(1)} %dynamic-slice_convert_fusion), channel_id=1, source_target_pairs={{0,16},{1,17},{2,18},{3,19},{4,20},{5,21},{6,22},{7,23},{8,24},{9,... | collective-permute-start | bytes 307208 | tf_op jit(solution)/shard_map/ppermute | solution.py:173
  19.9 4.7 %collective-permute-start.7 = (bf16[80,640]{1,0:T(8,128)(2,1)S(1)}, bf16[80,640]{1,0:T(8,128)(2,1)S(1)}, u32[]{:S(2)}, u32[]{:S(2)}) collective-permute-start(bf16[80,640]{1,0:T(8,128)(2,1)S(1)} %dynamic-slice_convert_fusion), channel_id=1, source_target_pairs={{0,8},{1,9},{2,10},{3,11},{4,12},{5,13},{6,14},{7,15},{8,0},{9,1},... | collective-permute-start | bytes 307208 | tf_op jit(solution)/shard_map/ppermute | solution.py:173
  20.0 28.2 %collective-permute-start.5 = (bf16[256,1280]{1,0:T(8,128)(2,1)}, bf16[256,1280]{1,0:T(8,128)(2,1)S(1)}, u32[]{:S(2)}, u32[]{:S(2)}) collective-permute-start(bf16[256,1280]{1,0:T(8,128)(2,1)} %l0.1), channel_id=1, source_target_pairs={{0,1},{1,0},{2,3},{3,2},{4,5},{5,4},{6,7},{7,6},{8,9},{9,8},{10,11... | collective-permute-start | bytes 1966088 | tf_op jit(solution)/shard_map/ppermute | solution.py:177
  24.6 7.4 %collective-permute-start.12 = (bf16[160,640]{1,0:T(8,128)(2,1)S(1)}, bf16[160,640]{1,0:T(8,128)(2,1)S(1)}, u32[]{:S(2)}, u32[]{:S(2)}) collective-permute-start(bf16[160,640]{1,0:T(8,128)(2,1)S(1)} %constant_dynamic-update-slice_fusion.wb), channel_id=1, source_target_pairs={{0,4},{1,5},{2,6},{3,7},{4,0},{5,1},{6,2},{7,3},{8,12},{9,13},{10,... | collective-permute-start | bytes 614408 | tf_op jit(solution)/shard_map/ppermute | solution.py:173
  26.1 5.8 %collective-permute-start.8 = (bf16[160,640]{1,0:T(8,128)(2,1)S(1)}, bf16[160,640]{1,0:T(8,128)(2,1)S(1)}, u32[]{:S(2)}, u32[]{:S(2)}) collective-permute-start(bf16[160,640]{1,0:T(8,128)(2,1)S(1)} %pad_maximum_fusion.2.wa), channel_id=1, source_target_pairs={{0,2},{1,3},{2,0},{3,1},{4,6},{5,7},{6,4},{7,5},{8,10},{9,11},{10,... | collective-permute-start | bytes 614408 | tf_op jit(solution)/shard_map/ppermute | solution.py:173
  32.0 16.2 %collective-permute-start.6 = (bf16[256,1280]{1,0:T(8,128)(2,1)}, bf16[256,1280]{1,0:T(8,128)(2,1)S(1)}, u32[]{:S(2)}, u32[]{:S(2)}) collective-permute-start(bf16[256,1280]{1,0:T(8,128)(2,1)} %n0.1), channel_id=1, source_target_pairs={{0,1},{1,0},{2,3},{3,2},{4,5},{5,4},{6,7},{7,6},{8,9},{9,8},{10,11... | collective-permute-start | bytes 1966088 | tf_op jit(solution)/shard_map/ppermute | solution.py:177
  32.0 24.5 %collective-permute-start.9 = (bf16[320,640]{1,0:T(8,128)(2,1)S(1)}, bf16[320,640]{1,0:T(8,128)(2,1)S(1)}, u32[]{:S(2)}, u32[]{:S(2)}) collective-permute-start(bf16[320,640]{1,0:T(8,128)(2,1)S(1)} %pad_maximum_fusion), channel_id=1, source_target_pairs={{0,4},{1,5},{2,6},{3,7},{4,0},{5,1},{6,2},{7,3},{8,12},{9,13},{10,... | collective-permute-start | bytes 1228808 | tf_op jit(solution)/shard_map/ppermute | solution.py:173
  32.6 23.9 %collective-permute-start.13 = (bf16[320,640]{1,0:T(8,128)(2,1)S(1)}, bf16[320,640]{1,0:T(8,128)(2,1)S(1)}, u32[]{:S(2)}, u32[]{:S(2)}) collective-permute-start(bf16[320,640]{1,0:T(8,128)(2,1)S(1)} %pad_maximum_fusion.1), channel_id=1, source_target_pairs={{0,2},{1,3},{2,0},{3,1},{4,6},{5,7},{6,4},{7,5},{8,10},{9,11},{10,... | collective-permute-start | bytes 1228808 | tf_op jit(solution)/shard_map/ppermute | solution.py:173
  34.2 10.2 %collective-permute-start.3 = (f32[1,1280]{1,0:T(1,128)S(1)}, f32[1,1280]{1,0:T(1,128)S(1)}, u32[]{:S(2)}, u32[]{:S(2)}) collective-permute-start(f32[1,1280]{1,0:T(1,128)S(1)} %add_add_fusion), channel_id=1, source_target_pairs={{0,2},{1,3},{2,0},{3,1},{4,6},{5,7},{6,4},{7,5},{8,10},{9,11},{10,... | collective-permute-start | bytes 15368 | tf_op jit(solution)/shard_map/ppermute | solution.py:173
  44.4 3.7 %collective-permute-start.4 = (f32[1,1280]{1,0:T(1,128)S(1)}, f32[1,1280]{1,0:T(1,128)S(1)}, u32[]{:S(2)}, u32[]{:S(2)}) collective-permute-start(f32[1,1280]{1,0:T(1,128)S(1)} %add.96), channel_id=1, source_target_pairs={{0,4},{1,5},{2,6},{3,7},{4,0},{5,1},{6,2},{7,3},{8,12},{9,13},{10,... | collective-permute-start | bytes 15368 | tf_op jit(solution)/shard_map/ppermute | solution.py:173
  59.6 9.7 %collective-permute-start.14 = (bf16[320,640]{1,0:T(8,128)(2,1)S(1)}, bf16[320,640]{1,0:T(8,128)(2,1)S(1)}, u32[]{:S(2)}, u32[]{:S(2)}) collective-permute-start(bf16[320,640]{1,0:T(8,128)(2,1)S(1)} %get-tuple-element.18), channel_id=1, source_target_pairs={{0,2},{1,3},{2,0},{3,1},{4,6},{5,7},{6,4},{7,5},{8,10},{9,11},{10,... | collective-permute-start | bytes 1228808 | tf_op jit(solution)/shard_map/ppermute | solution.py:173
  61.2 10.4 %collective-permute-start.17 = (bf16[320,640]{1,0:T(8,128)(2,1)S(1)}, bf16[320,640]{1,0:T(8,128)(2,1)S(1)}, u32[]{:S(2)}, u32[]{:S(2)}) collective-permute-start(bf16[320,640]{1,0:T(8,128)(2,1)S(1)} %get-tuple-element.20), channel_id=1, source_target_pairs={{0,4},{1,5},{2,6},{3,7},{4,0},{5,1},{6,2},{7,3},{8,12},{9,13},{10,... | collective-permute-start | bytes 1228808 | tf_op jit(solution)/shard_map/ppermute | solution.py:173
  69.5 5.8 %collective-permute-start.15 = (bf16[160,640]{1,0:T(8,128)(2,1)S(1)}, bf16[160,640]{1,0:T(8,128)(2,1)S(1)}, u32[]{:S(2)}, u32[]{:S(2)}) collective-permute-start(bf16[160,640]{1,0:T(8,128)(2,1)S(1)} %slice.58), channel_id=1, source_target_pairs={{0,4},{1,5},{2,6},{3,7},{4,0},{5,1},{6,2},{7,3},{8,12},{9,13},{10,... | collective-permute-start | bytes 614408 | tf_op jit(solution)/shard_map/ppermute | solution.py:173
  71.7 5.8 %collective-permute-start.18 = (bf16[160,640]{1,0:T(8,128)(2,1)S(1)}, bf16[160,640]{1,0:T(8,128)(2,1)S(1)}, u32[]{:S(2)}, u32[]{:S(2)}) collective-permute-start(bf16[160,640]{1,0:T(8,128)(2,1)S(1)} %slice.57), channel_id=1, source_target_pairs={{0,2},{1,3},{2,0},{3,1},{4,6},{5,7},{6,4},{7,5},{8,10},{9,11},{10,... | collective-permute-start | bytes 614408 | tf_op jit(solution)/shard_map/ppermute | solution.py:173
  75.3 21.9 %collective-permute-start.16 = (bf16[80,640]{1,0:T(8,128)(2,1)S(1)}, bf16[80,640]{1,0:T(8,128)(2,1)S(1)}, u32[]{:S(2)}, u32[]{:S(2)}) collective-permute-start(bf16[80,640]{1,0:T(8,128)(2,1)S(1)} %slice.59), channel_id=1, source_target_pairs={{0,8},{1,9},{2,10},{3,11},{4,12},{5,13},{6,14},{7,15},{8,0},{9,1},... | collective-permute-start | bytes 307208 | tf_op jit(solution)/shard_map/ppermute | solution.py:173
  77.6 19.7 %collective-permute-start.19 = (bf16[80,640]{1,0:T(8,128)(2,1)S(1)}, bf16[80,640]{1,0:T(8,128)(2,1)S(1)}, u32[]{:S(2)}, u32[]{:S(2)}) collective-permute-start(bf16[80,640]{1,0:T(8,128)(2,1)S(1)} %get-tuple-element.30), channel_id=1, source_target_pairs={{0,16},{1,17},{2,18},{3,19},{4,20},{5,21},{6,22},{7,23},{8,24},{9,... | collective-permute-start | bytes 307208 | tf_op jit(solution)/shard_map/ppermute | solution.py:173
  78.6 18.6 %collective-permute-start.20 = (bf16[80,640]{1,0:T(8,128)(2,1)S(1)}, bf16[80,640]{1,0:T(8,128)(2,1)S(1)}, u32[]{:S(2)}, u32[]{:S(2)}) collective-permute-start(bf16[80,640]{1,0:T(8,128)(2,1)S(1)} %get-tuple-element.31), channel_id=1, source_target_pairs={{0,24},{1,25},{2,26},{3,27},{4,28},{5,29},{6,30},{7,31},{8,16},{9,... | collective-permute-start | bytes 307208 | tf_op jit(solution)/shard_map/ppermute | solution.py:173
  81.5 3.7 %collective-permute-start.22 = (f32[1,1280]{1,0:T(1,128)S(1)}, f32[1,1280]{1,0:T(1,128)S(1)}, u32[]{:S(2)}, u32[]{:S(2)}) collective-permute-start(f32[1,1280]{1,0:T(1,128)S(1)} %shard_map.138), channel_id=1, source_target_pairs={{0,2},{1,3},{2,0},{3,1},{4,6},{5,7},{6,4},{7,5},{8,10},{9,11},{10,... | collective-permute-start | bytes 15368 | tf_op jit(solution)/shard_map/ppermute | solution.py:173
  85.2 3.7 %collective-permute-start.23 = (f32[1,1280]{1,0:T(1,128)S(1)}, f32[1,1280]{1,0:T(1,128)S(1)}, u32[]{:S(2)}, u32[]{:S(2)}) collective-permute-start(f32[1,1280]{1,0:T(1,128)S(1)} %add.110), channel_id=1, source_target_pairs={{0,4},{1,5},{2,6},{3,7},{4,0},{5,1},{6,2},{7,3},{8,12},{9,13},{10,... | collective-permute-start | bytes 15368 | tf_op jit(solution)/shard_map/ppermute | solution.py:173
  92.6 4.6 %collective-permute-start.25 = (f32[1,1280]{1,0:T(1,128)S(1)}, f32[1,1280]{1,0:T(1,128)S(1)}, u32[]{:S(2)}, u32[]{:S(2)}) collective-permute-start(f32[1,1280]{1,0:T(1,128)S(1)} %add.112), channel_id=1, source_target_pairs={{0,16},{1,17},{2,18},{3,19},{4,20},{5,21},{6,22},{7,23},{8,24},{9,... | collective-permute-start | bytes 15368 | tf_op jit(solution)/shard_map/ppermute | solution.py:173
  (11 other events, 212.6 us)

commit v2 on v1

--- a/solution.py
+++ b/solution.py
@@ -81,43 +81,115 @@
 
 
 VMEM = pl.BlockSpec(memory_space=pltpu.VMEM)
+ANY = pl.BlockSpec(memory_space=pl.ANY)
 SMEM = pl.BlockSpec(memory_space=pltpu.SMEM)
 
 
-def act_kernel(half, pos_ref, coef_ref, gain_ref, embed_ref, l0, n0, l1, n1, act_ref, slope_ref, diff_ref):
-    width = act_ref.shape[1]
-    col = pl.ds(pl.multiple_of(pos_ref[1] * half, 128), half)
+def split(x, parts):
+    out = []
+    for _ in range(parts):
+        top = x.astype(BF).astype(F32)
+        out.append(top)
+        x = x - top
+    return out
+
+
+def stack_rows(pieces, shape):
+    row = lax.broadcasted_iota(jnp.int32, shape, 0)
+    tile = jnp.zeros(shape, F32)
+    for i, piece in enumerate(pieces):
+        tile = jnp.where(row == i, jnp.broadcast_to(piece, shape), tile)
+    return tile
+
+
+def pack_kernel(w_ref, gain_ref, out_ref, part_ref, sem):
+    unit, half = part_ref.shape
+    col = pl.ds(pl.multiple_of(lax.axis_index("replica") * half, 128), half)
+    copy = pltpu.make_async_copy(w_ref.at[:, col], part_ref, sem)
+    copy.start()
+    out_ref[unit:, :] = jnp.zeros((16, half), BF)
+    gain = stack_rows(split(gain_ref[...], 3), (16, unit))
+    out_ref[unit:, :unit] = gain.astype(BF)
+    copy.wait()
+    out_ref[:unit, :] = part_ref[...].astype(BF)
+
+
+def norm_kernel(coef_ref, l_ref, n_ref, normed_ref, diff_ref):
+    rows, width = normed_ref.shape
+    half = width // 2
+    col = pl.ds(pl.multiple_of(lax.axis_index("replica") * half, 128), half)
     a, b = coef_ref[0], coef_ref[1]
+    tile = 32
+
+    def step(i, carry):
+        at = pl.ds(pl.multiple_of(i * tile, tile), tile)
+        noisy = a * l_ref[at, :].astype(F32) + b * n_ref[at, :].astype(F32)
+        mean = jnp.sum(noisy, axis=1, keepdims=True) * (1.0 / width)
+        cent = noisy - mean
+        var = jnp.sum(cent * cent, axis=1, keepdims=True) * (1.0 / width)
+        normed_ref[at, :] = cent * (1.0 / jnp.sqrt(var + 1e-05))
+        nh = n_ref[at, col].astype(F32)
+        diff_ref[at, :] = (a * l_ref[at, col].astype(F32) + b * nh) - nh
+        return carry
+
+    lax.fori_loop(0, rows // tile, step, 0)
+
+
+def join_kernel(unit, own, z1, after, wa):
+    wa[:unit, :] = own[:unit, :]
+    wa[unit:, :] = z1[:unit, :]
+
+
+def join_gain_kernel(unit, own, z1, z2, z3, after, wb, tile):
+    for i, z in enumerate((z2, z3)):
+        wb[i * unit : (i + 1) * unit, :] = z[:unit, :]
+    tile[...] = jnp.zeros_like(tile)
+    for i, z in enumerate((own, z1, z2, z3)):
+        tile[:, 128 * i : 128 * i + 128] = z[unit:, :128]
+    wb[2 * unit :, :] = tile[...]
+
+
+def pair_kernel(first, second, out):
+    n = out.shape[0] // 2
+    out[:n, :] = first[:n, :]
+    out[n:, :] = second[:n, :]
+
+
+def act_kernel(unit, embed_ref, t0, t1, t2, t3, normed0, normed1, act_ref, slope_ref, slots, gain_ref):
+    me = lax.axis_index("shard")
+    both, width = act_ref.shape
+    for kp, t in enumerate((t0, t1, t2, t3)):
+        x = t[...].astype(F32)
+        line = x[0:1, :] + x[1:2, :] + x[2:3, :]
+        for kz in range(4):
+            slots[4 * kz + kp : 4 * kz + kp + 1, :] = line[:, 128 * kz : 128 * kz + 128]
+    for i in range(16):
+        gain_ref[:, i * unit : (i + 1) * unit] = slots[pl.ds(me ^ i, 1), :unit]
     gain = gain_ref[...]
     embed = embed_ref[...]
-    tile = 16
-    for part, (l_ref, n_ref) in enumerate(((l0, n0), (l1, n1))):
-        rows = l_ref.shape[0]
-
-        def step(i, carry, l_ref=l_ref, n_ref=n_ref, base=part * rows):
+    tile = 32
+
+    for part, normed_ref in enumerate((normed0, normed1)):
+
+        def step(i, carry, normed_ref=normed_ref, base=part * normed0.shape[0]):
             at = pl.ds(pl.multiple_of(i * tile, tile), tile)
             to = pl.ds(pl.multiple_of(base + i * tile, tile), tile)
-            noisy = a * l_ref[at, :].astype(F32) + b * n_ref[at, :].astype(F32)
-            mean = jnp.sum(noisy, axis=1, keepdims=True) * (1.0 / width)
-            cent = noisy - mean
-            var = jnp.sum(cent * cent, axis=1, keepdims=True) * (1.0 / width)
-            normed = cent * (1.0 / jnp.sqrt(var + 1e-05))
+            normed = normed_ref[at, :]
             hidden = normed * gain + embed
-            sig = 1.0 / (1.0 + jnp.exp(-hidden))
-            act_ref[to, :] = (hidden * sig).astype(BF)
-            slope_ref[to, :] = sig * (1.0 + hidden * (1.0 - sig)) * normed
-            nh = n_ref[at, col].astype(F32)
-            diff_ref[to, :] = (a * l_ref[at, col].astype(F32) + b * nh) - nh
+            sig = 0.5 * jnp.tanh(0.5 * hidden) + 0.5
+            act = hidden * sig
+            act_ref[to, :] = act.astype(BF)
+            slope_ref[to, :] = (sig + act * (1.0 - sig)) * normed
             return carry
 
-        lax.fori_loop(0, rows // tile, step, 0)
+        lax.fori_loop(0, normed_ref.shape[0] // tile, step, 0)
 
 
 def mix_kernel(
-    scale, unit, pos_ref, act_ref, diff_ref, wa, wa1, wa2, wb, wb1, wb2,
-    gout_ref, w_ref, send_a, send_b, keep_a, keep_b, wg_ref,
+    scale, unit, act_ref, slope_ref, diff0, diff1, wa, wa1, wa2, wb, wb1, wb2,
+    send_a, send_b, keep_a, keep_b, keep_g, w_ref, wg_ref, gout_ref, slots,
 ):
-    me = pos_ref[0]
+    me = lax.axis_index("shard")
 
     def place(kz, kp):
         return pl.ds(pl.multiple_of((me ^ (kz * 4 + kp)) * unit, 16), unit)
@@ -135,10 +207,27 @@
         w_ref[place(2 + k, 1), :] = wb2[rows(k), :]
         w_ref[place(2 + k, 3), :] = wb2[rows(2 + k), :]
     product = jnp.dot(act_ref[...], w_ref[...], preferred_element_type=F32)
-    gout_ref[...] = ((diff_ref[...] + product) * scale).astype(BF)
+    own_rows = diff0.shape[0]
+    gout_ref[:own_rows, :] = ((diff0[...] + product[:own_rows]) * scale).astype(BF)
+    gout_ref[own_rows:, :] = ((diff1[...] + product[own_rows:]) * scale).astype(BF)
+    grad_act = lax.dot_general(
+        gout_ref[...], w_ref[...], (((1,), (1,)), ((), ())), preferred_element_type=F32
+    )
+    part = jnp.sum(grad_act * slope_ref[...], axis=0, keepdims=True)
     wg_ref[...] = lax.dot_general(
         act_ref[...], gout_ref[...], (((0,), (0,)), ((), ())), preferred_element_type=F32
     )
+    half = wg_ref.shape[1]
+    slots[...] = jnp.zeros_like(slots)
+    for i in range(16):
+        slots[pl.ds(me ^ i, 1), :unit] = part[:, i * unit : (i + 1) * unit]
+    lines = [
+        jnp.concatenate([slots[4 * kz + kp : 4 * kz + kp + 1, :] for kz in range(4)], axis=1)
+        for kp in range(4)
+    ]
+    keep_g[...] = jnp.zeros_like(keep_g)
+    keep_g[0:1, :512] = lines[0]
+    keep_g[1:2, :512] = lines[2]
     for k in range(2):
         send_a[rows(k), :] = wg_ref[place(k, 1), :].astype(BF)
         send_a[rows(2 + k), :] = wg_ref[place(k, 3), :].astype(BF)
@@ -148,13 +237,71 @@
         send_b[rows(2 + k), :] = wg_ref[place(2 + k, 3), :].astype(BF)
         keep_b[rows(k), :] = wg_ref[place(2 + k, 0), :]
         keep_b[rows(2 + k), :] = wg_ref[place(2 + k, 1), :]
-
-
-def gain_kernel(gout_ref, w_ref, slope_ref, out_ref):
-    grad_act = lax.dot_general(
-        gout_ref[...], w_ref[...], (((1,), (1,)), ((), ())), preferred_element_type=F32
-    )
-    out_ref[...] = jnp.sum(grad_act * slope_ref[...], axis=0, keepdims=True)
+    send_a[4 * unit :, :] = jnp.zeros((16, half), BF)
+    send_a[4 * unit :, :512] = stack_rows(split(lines[1], 2) + split(lines[3], 2), (16, 512)).astype(BF)
+
+
+def fold_a_kernel(unit, keep_a, keep_g, got, send, own, own_g):
+    two = 2 * unit
+    send[:two, :] = (keep_a[two:, :] + got[two : 2 * two, :].astype(F32)).astype(BF)
+    extra = got[2 * two :, :].astype(F32)
+    own_g[...] = jnp.zeros_like(own_g)
+    own_g[0:1, :] = keep_g[0:1, :] + (extra[0:1, :] + extra[1:2, :])
+    line = keep_g[1:2, :] + (extra[2:3, :] + extra[3:4, :])
+    send[two:, :] = stack_rows(split(line, 2), (16, line.shape[1])).astype(BF)
+    own[...] = keep_a[:two, :] + got[:two, :].astype(F32)
+
+
+def fold_b_kernel(unit, keep_b, got, send, own):
+    two = 2 * unit
+    send[...] = (keep_b[two:, :] + got[two:, :].astype(F32)).astype(BF)
+    own[...] = keep_b[:two, :] + got[:two, :].astype(F32)
+
+
+def turn_a_kernel(unit, own, own_g, got, send1, mine, line_ref):
+    two = 2 * unit
+    half = own.shape[1]
+    extra = got[two:, :].astype(F32)
+    line = own_g[0:1, :] + (extra[0:1, :] + extra[1:2, :])
+    send1[:unit, :] = (own[unit:, :] + got[unit:two, :].astype(F32)).astype(BF)
+    send1[unit:, :] = jnp.zeros((16, half), BF)
+    send1[unit:, :128] = stack_rows(split(line[:, 128:256], 2), (16, 128)).astype(BF)
+    mine[...] = own[:unit, :] + got[:unit, :].astype(F32)
+    line_ref[...] = jnp.zeros_like(line_ref)
+    line_ref[0:1, :] = line
+
+
+def turn_b_kernel(unit, own, got, line_ref, send2, send3):
+    half = own.shape[1]
+    total = own[...] + got[...].astype(F32)
+    for k, send in ((2, send2), (3, send3)):
+        send[:unit, :] = total[(k - 2) * unit : (k - 1) * unit, :].astype(BF)
+        send[unit:, :] = jnp.zeros((16, half), BF)
+        piece = line_ref[0:1, 128 * k : 128 * k + 128]
+        send[unit:, :128] = stack_rows(split(piece, 2), (16, 128)).astype(BF)
+
+
+def last_kernel(unit, mine, line_ref, h1, h2, h3, out_ref):
+    total = mine[...]
+    line = line_ref[0:1, :128]
+    for h in (h1, h2, h3):
+        total = total + h[:unit, :].astype(F32)
+        extra = h[unit:, :128].astype(F32)
+        line = line + (extra[0:1, :] + extra[1:2, :])
+    out_ref[:unit, :] = total
+    out_ref[unit:, :] = jnp.zeros((8, total.shape[1]), F32)
+    out_ref[unit : unit + 1, :128] = line
+
+
+def adam_kernel(unit, half, mine, theirs, w, wm, ws, g, gm, gs, nw, nwm, nws, ng, ngm, ngs):
+    core = lax.axis_index("replica")
+    for ref, side in ((mine, core), (theirs, 1 - core)):
+        col = pl.ds(pl.multiple_of(side * half, 128), half)
+        nw[:, col], nwm[:, col], nws[:, col] = adam_step(
+            w[:, col], ref[:unit, :], wm[:, col], ws[:, col]
+        )
+    line = mine[unit : unit + 1, :unit] + theirs[unit : unit + 1, :unit]
+    ng[...], ngm[...], ngs[...] = adam_step(g[...], line, gm[...], gs[...])
 
 
 def paired_body(
@@ -165,8 +312,8 @@
     shards, cores = lax.axis_size("shard"), lax.axis_size("replica")
     total_rows = rows * shards * cores
     half = width // 2
-    me, core = lax.axis_index("shard"), lax.axis_index("replica")
-    pos = jnp.stack([me, core]).astype(jnp.int32)
+    both = rows * cores
+    me = lax.axis_index("shard")
 
     def to(x, k):
         pairs = [(i * cores + c, (i ^ k) * cores + c) for i in range(shards) for c in range(cores)]
@@ -188,22 +335,16 @@
         )
 
     arr = jax.ShapeDtypeStruct
-
-    own = lax.dynamic_slice(master_weight, (0, core * half), (unit, half)).astype(BF)
+    two, four = 2 * unit, 4 * unit
+
+    own = call(
+        pack_kernel,
+        arr((unit + 16, half), BF),
+        [ANY, VMEM],
+        [pltpu.VMEM((unit, half), F32), pltpu.SemaphoreType.DMA],
+        byts=6 * unit * half,
+    )(master_weight, norm_gain.reshape(1, unit))
     z1, z2, z3 = to(own, 4), to(own, 8), to(own, 12)
-    wa = jnp.concatenate([own, z1], axis=0)
-    wa1 = to(wa, 1)
-    wb = jnp.concatenate([z2, z3], axis=0)
-    wb1 = to(wb, 2)
-    wa2 = to(jnp.concatenate([wa, wa1], axis=0), 2)
-    wb2 = to(jnp.concatenate([wb, wb1], axis=0), 1)
-
-    gain = lax.dynamic_update_slice(
-        jnp.zeros((1, width), F32), norm_gain.reshape(1, unit), (0, me * unit)
-    )
-    gain = gain + to(gain, 4) + to(gain, 8) + to(gain, 12)
-    gain = gain + to(gain, 1)
-    gain = gain + to(gain, 2)
 
     other_latents, other_noise = across(latents), across(noise)
     step_time = lax.dynamic_slice(timesteps, (me * cores * rows // VOX,), (1,)).astype(F32)
@@ -211,67 +352,112 @@
     coef = jnp.concatenate([jnp.sqrt(level), jnp.sqrt(1.0 - level)])
     angles = step_time[:, None] * frequencies(width)[None, :]
     embed = jnp.concatenate([jnp.sin(angles), jnp.cos(angles)], axis=1)
-    both = rows * cores
-    act, slope, diff = call(
-        functools.partial(act_kernel, half),
-        (arr((both, width), BF), arr((both, width), F32), arr((both, half), F32)),
-        [SMEM, SMEM] + [VMEM] * 6,
-        flops=30 * both * width,
+    normalize = call(
+        norm_kernel,
+        (arr((rows, width), F32), arr((rows, half), F32)),
+        [SMEM] + [VMEM] * 2,
+        flops=10 * rows * width,
+        byts=8 * rows * width,
+    )
+    normed0, diff0 = normalize(coef, latents, noise)
+    normed1, diff1 = normalize(coef, other_latents, other_noise)
+
+    wa = call(
+        functools.partial(join_kernel, unit),
+        arr((two, half), BF),
+        [VMEM] * 2 + [ANY],
+        byts=8 * unit * half,
+    )(own, z1, diff0)
+    wa1 = to(wa, 1)
+    wb, gain_tile = call(
+        functools.partial(join_gain_kernel, unit),
+        (arr((two + 16, half), BF), arr((16, half), BF)),
+        [VMEM] * 4 + [ANY],
+        byts=8 * unit * half,
+    )(own, z1, z2, z3, diff1)
+    wb1 = to(wb, 2)
+    gain_x, gain_xy = to(gain_tile, 1), to(gain_tile, 3)
+    pair = call(pair_kernel, arr((four, half), BF), [VMEM] * 2, byts=16 * unit * half)
+    wa2 = to(pair(wa, wa1), 2)
+    wb2 = to(pair(wb, wb1), 1)
+    gain_y = wb1[two:]
+    act, slope = call(
+        functools.partial(act_kernel, unit),
+        (arr((both, width), BF), arr((both, width), F32)),
+        [VMEM] * 7,
+        [pltpu.VMEM((16, 128), F32), pltpu.VMEM((1, width), F32)],
+        flops=20 * both * width,
         byts=8 * both * width,
-    )(pos, coef, gain, embed, latents, noise, other_latents, other_noise)
-
-    gout, mixing, send_a, send_b, keep_a, keep_b = call(
+    )(embed, gain_tile, gain_x, gain_y, gain_xy, normed0, normed1)
+
+    send_a, send_b, keep_a, keep_b, keep_g = call(
         functools.partial(mix_kernel, 1.0 / math.sqrt(total_rows), unit),
         (
-            arr((both, half), BF),
-            arr((width, half), BF),
-            arr((4 * unit, half), BF),
-            arr((4 * unit, half), BF),
-            arr((4 * unit, half), F32),
-            arr((4 * unit, half), F32),
+            arr((four + 16, half), BF),
+            arr((four, half), BF),
+            arr((four, half), F32),
+            arr((four, half), F32),
+            arr((8, half), F32),
         ),
-        [SMEM] + [VMEM] * 8,
-        [pltpu.VMEM((width, half), F32)],
-        flops=4 * both * width * half,
+        [VMEM] * 10,
+        [
+            pltpu.VMEM((width, half), BF),
+            pltpu.VMEM((width, half), F32),
+            pltpu.VMEM((both, half), BF),
+            pltpu.VMEM((16, 128), F32),
+        ],
+        flops=6 * both * width * half,
         byts=6 * both * width,
-    )(pos, act, diff, wa, wa1, wa2, wb, wb1, wb2)
+    )(act, slope, diff0, diff1, wa, wa1, wa2, wb, wb1, wb2)
 
     got_a, got_b = to(send_a, 1), to(send_b, 2)
-    part = call(
-        gain_kernel,
-        arr((1, width), F32),
+    send_a, own_a, own_g = call(
+        functools.partial(fold_a_kernel, unit),
+        (arr((two + 16, half), BF), arr((two, half), F32), arr((8, half), F32)),
         [VMEM] * 3,
-        flops=2 * both * width * half,
-        byts=6 * both * width,
-    )(gout, mixing, slope)
-
-    two, one = 2 * unit, unit
-    sum_a = keep_a + got_a.astype(F32)
-    sum_b = keep_b + got_b.astype(F32)
-    got_a2 = to(sum_a[two:].astype(BF), 2)
-    got_b2 = to(sum_b[two:].astype(BF), 1)
-    sum_a = sum_a[:two] + got_a2.astype(F32)
-    sum_b = sum_b[:two] + got_b2.astype(F32)
-    h1 = to(sum_a[one:].astype(BF), 4)
-    h2 = to(sum_b[:one].astype(BF), 8)
-    h3 = to(sum_b[one:].astype(BF), 12)
-    mine = sum_a[:one] + h1.astype(F32) + h2.astype(F32) + h3.astype(F32)
-
-    for k in (1, 2, 4, 8):
-        part = part + to(part, k)
-    part = part + across(part)
-    gain_grad = lax.dynamic_slice(part, (0, me * unit), (1, unit)).reshape(unit)
-
+        byts=8 * four * half,
+    )(keep_a, keep_g, got_a)
+    got_a = to(send_a, 2)
+    send_b, own_b = call(
+        functools.partial(fold_b_kernel, unit),
+        (arr((two, half), BF), arr((two, half), F32)),
+        [VMEM] * 2,
+        byts=8 * four * half,
+    )(keep_b, got_b)
+    got_b = to(send_b, 1)
+    send1, mine, line = call(
+        functools.partial(turn_a_kernel, unit),
+        (arr((unit + 16, half), BF), arr((unit, half), F32), arr((8, half), F32)),
+        [VMEM] * 3,
+        byts=8 * two * half,
+    )(own_a, own_g, got_a)
+    h1 = to(send1, 4)
+    send2, send3 = call(
+        functools.partial(turn_b_kernel, unit),
+        (arr((unit + 16, half), BF), arr((unit + 16, half), BF)),
+        [VMEM] * 3,
+        byts=8 * two * half,
+    )(own_b, got_b, line)
+    h2, h3 = to(send2, 8), to(send3, 12)
+    mine = call(
+        functools.partial(last_kernel, unit),
+        arr((unit + 8, half), F32),
+        [VMEM] * 5,
+        byts=16 * unit * half,
+    )(mine, line, h1, h2, h3)
     theirs = across(mine)
-    weight_grad = jnp.where(
-        core == 0,
-        jnp.concatenate([mine, theirs], axis=1),
-        jnp.concatenate([theirs, mine], axis=1),
-    )
-    return (
-        *adam_step(master_weight, weight_grad, weight_moment, weight_second),
-        *adam_step(norm_gain, gain_grad, gain_moment, gain_second),
-    )
+    flat = arr((unit, width), F32)
+    thin = arr((1, unit), F32)
+    *weights, ng, ngm, ngs = call(
+        functools.partial(adam_kernel, unit, half),
+        (flat, flat, flat, thin, thin, thin),
+        [VMEM] * 8,
+        byts=24 * unit * width,
+    )(
+        mine, theirs, master_weight, weight_moment, weight_second,
+        *(x.reshape(1, unit) for x in (norm_gain, gain_moment, gain_second)),
+    )
+    return (*weights, ng.reshape(unit), ngm.reshape(unit), ngs.reshape(unit))
 
 
 def body(latents, *rest):
@@ -281,7 +467,9 @@
         lax.axis_size("shard") == 16
         and lax.axis_size("replica") == 2
         and unit % 16 == 0
+        and unit <= 128
         and width % 256 == 0
+        and width >= 1024
         and rows % 16 == 0
         and VOX % (2 * rows) == 0
     )

time: 100 us -> 76.3 us (0.76)
  waiting for transfers between devices: 47.2 us -> 34.8 us
  starting transfers between devices: 32 us -> 24.8 us
  other arithmetic: 3.28 us -> 0.18 us
  Pallas kernels: 12.7 us -> 11.7 us
    ppermute x23 -> x16, waiting for transfers between devices: 46.7 us -> 33.3 us  [to(): return lax.ppermute(x, AXES, pairs)]
    ppermute x23 -> x16, starting transfers between devices: 31.3 us -> 24.1 us  [to(): return lax.ppermute(x, AXES, pairs)]
    sub x2 -> x0, other arithmetic: 1.84 us -> none  [adam_step(): return (param - 0.05 * update, new_moment, new_second)]
    unnamed x17 -> x20, local copies, waits for them, and re-layouts: 0.05 us -> 1.71 us
    pallas_call x2 -> x14, Pallas kernels: 9.61 us -> 8.05 us  [the longest x1 2.49 us: paired_body(): normed1, diff1 = normalize(coef, other_latents, other_noise)]
  transfers between devices with their start and end apart: 27 -> 19, of which waited for: 14 -> 12; matrix products, arithmetic and copies ran while one was open for 4% -> 2% of each run, Pallas kernels for 10% -> 9%
where the time goes in v2:
time: 76.3 us; the launch traced here: 76.1 us
  waiting for transfers between devices  34.8 us (46%)
  starting transfers between devices  24.8 us (33%)
  Pallas kernels  11.7 us (15%)
  local copies, waits for them, and re-layouts  2.95 us (4%)
  between operations  1.67 us (2%)
    ppermute x16, waiting for transfers between devices, to(): return lax.ppermute(x, AXES, pairs)  33.3 us
    ppermute x16, starting transfers between devices, to(): return lax.ppermute(x, AXES, pairs)  24.1 us
    pallas_call x1, Pallas kernels, paired_body(): call(functools.partial(mix_kernel, 1.0 / math.sqrt(total_rows), unit), (a...  3.66 us
    pallas_call x1, Pallas kernels, paired_body(): normed1, diff1 = normalize(coef, other_latents, other_noise)  2.49 us
    pallas_call x1, Pallas kernels, paired_body(): normed0, diff0 = normalize(coef, latents, noise)  2.49 us
    unnamed x20, local copies, waits for them, and re-layouts  1.71 us
  transfers between devices with their start and end apart: 19, of which 12 were waited for; matrix products, arithmetic and copies ran while one was open for 2% of the time, Pallas kernels for 9%

profile of v2, /device:TPU:0, one launch (start us, length us, event | category | flops | bytes accessed | tf_op | source)
XLA Modules:
  0.0 76.1 jit_solution(10136467540917819391)
XLA Ops:
  3.0 3.1 %collective-permute-start = (bf16[96,640]{1,0:T(8,128)(2,1)S(1)}, bf16[96,640]{1,0:T(8,128)(2,1)S(1)}, u32[]{:S(2)}, u32[]{:S(2)}) collective-permute-start(bf16[96,640]{1,0:T(8,128)(2,1)S(1)} %shard_map.136.own), channel_id=1, source_target_pairs={{0,8},{1,9},{2,10},{3,11},{4,12},{5,13},{6,14},{7,15},{8,0},{9,1},... | collective-permute-start | bytes 368648 | tf_op jit(solution)/shard_map/ppermute | solution.py:320
  6.0 2.6 %collective-permute-start.1 = (bf16[96,640]{1,0:T(8,128)(2,1)S(1)}, bf16[96,640]{1,0:T(8,128)(2,1)S(1)}, u32[]{:S(2)}, u32[]{:S(2)}) collective-permute-start(bf16[96,640]{1,0:T(8,128)(2,1)S(1)} %shard_map.136.own), channel_id=1, source_target_pairs={{0,16},{1,17},{2,18},{3,19},{4,20},{5,21},{6,22},{7,23},{8,24},{9,... | collective-permute-start | bytes 368648 | tf_op jit(solution)/shard_map/ppermute | solution.py:320
  8.6 1.2 %dynamic_slice.3 = s32[1]{0:T(128)} dynamic-slice(s32[16]{0:T(128)} %param.11, s32[]{:T(128)S(6)} %select_n.9), dynamic_slice_sizes={1} | dynamic-slice | bytes 12 | tf_op jit(solution)/shard_map/dynamic_slice | solution.py:350
  10.8 2.5 %shard_map.137 = (f32[256,1280]{1,0:T(8,128)S(1)}, f32[256,640]{1,0:T(8,128)S(1)}) custom-call(f32[2]{0:T(128)S(1)} %pad_maximum_fusion.1.coef_ref, bf16[256,1280]{1,0:T(8,128)(2,1)S(1)} %collective-permute-done.3.l_ref, bf16[256,1280]{1,0:T(8,128)(2,1)S(1)} %collective-permute-done.4.n_ref), custom_call_target="tpu_custom_call" | custom-call | flops 3276800 | bytes 2621440 | tf_op jit(solution)/shard_map/pallas_call | solution.py:363
  13.3 5.1 %collective-permute-done.1.z2 = bf16[96,640]{1,0:T(8,128)(2,1)S(1)} collective-permute-done((bf16[96,640]{1,0:T(8,128)(2,1)S(1)}, bf16[96,640]{1,0:T(8,128)(2,1)S(1)}, u32[]{:S(2)}, u32[]{:S(2)}) %collective-permute-start.1) | collective-permute-done | bytes 122912 | tf_op jit(solution)/shard_map/ppermute | solution.py:320
  18.5 1.6 %collective-permute-start.6 = (bf16[176,640]{1,0:T(8,128)(2,1)S(1)}, bf16[176,640]{1,0:T(8,128)(2,1)S(1)}, u32[]{:S(2)}, u32[]{:S(2)}) collective-permute-start(bf16[176,640]{1,0:T(8,128)(2,1)S(1)} %get-tuple-element.37.first.wb), channel_id=1, source_target_pairs={{0,4},{1,5},{2,6},{3,7},{4,0},{5,1},{6,2},{7,3},{8,12},{9,13},{10,... | collective-permute-start | bytes 675848 | tf_op jit(solution)/shard_map/ppermute | solution.py:320
  20.0 2.5 %shard_map.139 = (f32[256,1280]{1,0:T(8,128)S(1)}, f32[256,640]{1,0:T(8,128)S(1)}) custom-call(f32[2]{0:T(128)S(1)} %pad_maximum_fusion.1.coef_ref, bf16[256,1280]{1,0:T(8,128)(2,1)S(1)} %copy-done.2, bf16[256,1280]{1,0:T(8,128)(2,1)S(1)} %copy-done.3), custom_call_target="tpu_custom_call" | custom-call | flops 3276800 | bytes 2621440 | tf_op jit(solution)/shard_map/pallas_call | solution.py:362
  22.6 1.6 %collective-permute-start.8 = (bf16[160,640]{1,0:T(8,128)(2,1)S(1)}, bf16[160,640]{1,0:T(8,128)(2,1)S(1)}, u32[]{:S(2)}, u32[]{:S(2)}) collective-permute-start(bf16[160,640]{1,0:T(8,128)(2,1)S(1)} %shard_map.141.first.wa), channel_id=1, source_target_pairs={{0,2},{1,3},{2,0},{3,1},{4,6},{5,7},{6,4},{7,5},{8,10},{9,11},{10,... | collective-permute-start | bytes 614408 | tf_op jit(solution)/shard_map/ppermute | solution.py:320
  24.1 4.4 %collective-permute-done.8.second.wa1 = bf16[160,640]{1,0:T(8,128)(2,1)S(1)} collective-permute-done((bf16[160,640]{1,0:T(8,128)(2,1)S(1)}, bf16[160,640]{1,0:T(8,128)(2,1)S(1)}, u32[]{:S(2)}, u32[]{:S(2)}) %collective-permute-start.8) | collective-permute-done | bytes 204832 | tf_op jit(solution)/shard_map/ppermute | solution.py:320
  29.0 1.6 %collective-permute-start.10 = (bf16[320,640]{1,0:T(8,128)(2,1)S(1)}, bf16[320,640]{1,0:T(8,128)(2,1)S(1)}, u32[]{:S(2)}, u32[]{:S(2)}) collective-permute-start(bf16[320,640]{1,0:T(8,128)(2,1)S(1)} %shard_map.143), channel_id=1, source_target_pairs={{0,2},{1,3},{2,0},{3,1},{4,6},{5,7},{6,4},{7,5},{8,10},{9,11},{10,... | collective-permute-start | bytes 1228808 | tf_op jit(solution)/shard_map/ppermute | solution.py:320
  31.3 2.6 %collective-permute-start.7 = (bf16[16,640]{1,0:T(8,128)(2,1)S(1)}, bf16[16,640]{1,0:T(8,128)(2,1)S(1)}, u32[]{:S(2)}, u32[]{:S(2)}) collective-permute-start(bf16[16,640]{1,0:T(8,128)(2,1)S(1)} %get-tuple-element.36.t0), channel_id=1, source_target_pairs={{0,6},{1,7},{2,4},{3,5},{4,2},{5,3},{6,0},{7,1},{8,14},{9,15},{10,... | collective-permute-start | bytes 61448 | tf_op jit(solution)/shard_map/ppermute | solution.py:320
  33.9 4.0 %collective-permute-done.5.t1 = bf16[16,640]{1,0:T(8,128)(2,1)S(1)} collective-permute-done((bf16[16,640]{1,0:T(8,128)(2,1)S(1)}, bf16[16,640]{1,0:T(8,128)(2,1)S(1)}, u32[]{:S(2)}, u32[]{:S(2)}) %collective-permute-start.5) | collective-permute-done | bytes 20512 | tf_op jit(solution)/shard_map/ppermute | solution.py:320
  39.8 3.7 %shard_map.144 = (bf16[336,640]{1,0:T(8,128)(2,1)S(1)}, bf16[320,640]{1,0:T(8,128)(2,1)S(1)}, f32[320,640]{1,0:T(8,128)S(1)}, f32[320,640]{1,0:T(8,128)S(1)}, f32[8,640]{1,0:T(8,128)S(1)}) custom-call(bf16[512,1280]{1,0:T(8,128)(2,1)S(1)} %get-tuple-element.40.act_ref, f32[512,1280]{1,0:T(8,128)S(1)} %get-tuple-element.41.slope_ref, ...), custom_call_target="tpu_custom_call" | custom-call | flops 2516582400 | bytes 3932160 | tf_op jit(solution)/shard_map/pallas_call | solution.py:393
  43.5 1.6 %collective-permute-start.11 = (bf16[336,640]{1,0:T(8,128)(2,1)S(1)}, bf16[336,640]{1,0:T(8,128)(2,1)S(1)}, u32[]{:S(2)}, u32[]{:S(2)}) collective-permute-start(bf16[336,640]{1,0:T(8,128)(2,1)S(1)} %get-tuple-element.45), channel_id=1, source_target_pairs={{0,2},{1,3},{2,0},{3,1},{4,6},{5,7},{6,4},{7,5},{8,10},{9,11},{10,... | collective-permute-start | bytes 1290248 | tf_op jit(solution)/shard_map/ppermute | solution.py:320
  46.0 7.7 %collective-permute-done.11.got = bf16[336,640]{1,0:T(8,128)(2,1)S(1)} collective-permute-done((bf16[336,640]{1,0:T(8,128)(2,1)S(1)}, bf16[336,640]{1,0:T(8,128)(2,1)S(1)}, u32[]{:S(2)}, u32[]{:S(2)}) %collective-permute-start.11) | collective-permute-done | bytes 430112 | tf_op jit(solution)/shard_map/ppermute | solution.py:320
  55.4 1.4 %collective-permute-start.15 = (bf16[160,640]{1,0:T(8,128)(2,1)S(1)}, bf16[160,640]{1,0:T(8,128)(2,1)S(1)}, u32[]{:S(2)}, u32[]{:S(2)}) collective-permute-start(bf16[160,640]{1,0:T(8,128)(2,1)S(1)} %get-tuple-element.55), channel_id=1, source_target_pairs={{0,2},{1,3},{2,0},{3,1},{4,6},{5,7},{6,4},{7,5},{8,10},{9,11},{10,... | collective-permute-start | bytes 614408 | tf_op jit(solution)/shard_map/ppermute | solution.py:320
  56.8 3.1 %collective-permute-done.12.got = bf16[176,640]{1,0:T(8,128)(2,1)S(1)} collective-permute-done((bf16[176,640]{1,0:T(8,128)(2,1)S(1)}, bf16[176,640]{1,0:T(8,128)(2,1)S(1)}, u32[]{:S(2)}, u32[]{:S(2)}) %collective-permute-start.12) | collective-permute-done | bytes 225312 | tf_op jit(solution)/shard_map/ppermute | solution.py:320
  59.9 1.3 %collective-permute-done.15.got = bf16[160,640]{1,0:T(8,128)(2,1)S(1)} collective-permute-done((bf16[160,640]{1,0:T(8,128)(2,1)S(1)}, bf16[160,640]{1,0:T(8,128)(2,1)S(1)}, u32[]{:S(2)}, u32[]{:S(2)}) %collective-permute-start.15) | collective-permute-done | bytes 204832 | tf_op jit(solution)/shard_map/ppermute | solution.py:320
  61.2 4.4 %collective-permute-start.16 = (bf16[96,640]{1,0:T(8,128)(2,1)S(1)}, bf16[96,640]{1,0:T(8,128)(2,1)S(1)}, u32[]{:S(2)}, u32[]{:S(2)}) collective-permute-start(bf16[96,640]{1,0:T(8,128)(2,1)S(1)} %get-tuple-element.56), channel_id=1, source_target_pairs={{0,16},{1,17},{2,18},{3,19},{4,20},{5,21},{6,22},{7,23},{8,24},{9,... | collective-permute-start | bytes 368648 | tf_op jit(solution)/shard_map/ppermute | solution.py:320
  65.6 1.3 %collective-permute-start.17 = (bf16[96,640]{1,0:T(8,128)(2,1)S(1)}, bf16[96,640]{1,0:T(8,128)(2,1)S(1)}, u32[]{:S(2)}, u32[]{:S(2)}) collective-permute-start(bf16[96,640]{1,0:T(8,128)(2,1)S(1)} %get-tuple-element.57), channel_id=1, source_target_pairs={{0,24},{1,25},{2,26},{3,27},{4,28},{5,29},{6,30},{7,31},{8,16},{9,... | collective-permute-start | bytes 368648 | tf_op jit(solution)/shard_map/ppermute | solution.py:320
  66.9 1.6 %collective-permute-done.16.h2 = bf16[96,640]{1,0:T(8,128)(2,1)S(1)} collective-permute-done((bf16[96,640]{1,0:T(8,128)(2,1)S(1)}, bf16[96,640]{1,0:T(8,128)(2,1)S(1)}, u32[]{:S(2)}, u32[]{:S(2)}) %collective-permute-start.16) | collective-permute-done | bytes 122912 | tf_op jit(solution)/shard_map/ppermute | solution.py:320
  68.5 4.0 %collective-permute-done.17.h3 = bf16[96,640]{1,0:T(8,128)(2,1)S(1)} collective-permute-done((bf16[96,640]{1,0:T(8,128)(2,1)S(1)}, bf16[96,640]{1,0:T(8,128)(2,1)S(1)}, u32[]{:S(2)}, u32[]{:S(2)}) %collective-permute-start.17) | collective-permute-done | bytes 122912 | tf_op jit(solution)/shard_map/ppermute | solution.py:320
  73.3 1.5 %collective-permute-done.18.theirs = f32[88,640]{1,0:T(8,128)S(1)} collective-permute-done((f32[88,640]{1,0:T(8,128)S(1)}, f32[88,640]{1,0:T(8,128)S(1)}, u32[]{:S(2)}, u32[]{:S(2)}) %collective-permute-start.18) | collective-permute-done | bytes 225312 | tf_op jit(solution)/shard_map/ppermute | solution.py:324
  74.8 1.3 %shard_map.150 = (f32[80,1280]{1,0:T(8,128)}, f32[80,1280]{1,0:T(8,128)}, f32[80,1280]{1,0:T(8,128)}, f32[1,80]{1,0:T(1,128)}, f32[1,80]{1,0:T(1,128)}, /*index=5*/f32[1,80]{1,0:T(1,128)}) custom-call(f32[88,640]{1,0:T(8,128)S(1)} %shard_map.149.mine, f32[88,640]{1,0:T(8,128)S(1)} %collective-permute-done.18.theirs, f32[80,1280]{1,0:T(8,128)S(1)} %copy-done.1, ...), custom_call_target="tpu_custom_call" | custom-call | bytes 2457600 | tf_op jit(solution)/shard_map/pallas_call | solution.py:451
  (54 shorter events, 9.2 us)
Async XLA Ops:
  0.6 10.1 %collective-permute-start.3 = (bf16[256,1280]{1,0:T(8,128)(2,1)}, bf16[256,1280]{1,0:T(8,128)(2,1)S(1)}, u32[]{:S(2)}, u32[]{:S(2)}) collective-permute-start(bf16[256,1280]{1,0:T(8,128)(2,1)} %l_ref.1), channel_id=1, source_target_pairs={{0,1},{1,0},{2,3},{3,2},{4,5},{5,4},{6,7},{7,6},{8,9},{9,8},{10,11... | collective-permute-start | bytes 1966088 | tf_op jit(solution)/shard_map/ppermute | solution.py:324
  1.1 9.6 %collective-permute-start.4 = (bf16[256,1280]{1,0:T(8,128)(2,1)}, bf16[256,1280]{1,0:T(8,128)(2,1)S(1)}, u32[]{:S(2)}, u32[]{:S(2)}) collective-permute-start(bf16[256,1280]{1,0:T(8,128)(2,1)} %n_ref.1), channel_id=1, source_target_pairs={{0,1},{1,0},{2,3},{3,2},{4,5},{5,4},{6,7},{7,6},{8,9},{9,8},{10,11... | collective-permute-start | bytes 1966088 | tf_op jit(solution)/shard_map/ppermute | solution.py:324
  3.0 10.3 %collective-permute-start = (bf16[96,640]{1,0:T(8,128)(2,1)S(1)}, bf16[96,640]{1,0:T(8,128)(2,1)S(1)}, u32[]{:S(2)}, u32[]{:S(2)}) collective-permute-start(bf16[96,640]{1,0:T(8,128)(2,1)S(1)} %shard_map.136.own), channel_id=1, source_target_pairs={{0,8},{1,9},{2,10},{3,11},{4,12},{5,13},{6,14},{7,15},{8,0},{9,1},... | collective-permute-start | bytes 368648 | tf_op jit(solution)/shard_map/ppermute | solution.py:320
  6.0 12.4 %collective-permute-start.1 = (bf16[96,640]{1,0:T(8,128)(2,1)S(1)}, bf16[96,640]{1,0:T(8,128)(2,1)S(1)}, u32[]{:S(2)}, u32[]{:S(2)}) collective-permute-start(bf16[96,640]{1,0:T(8,128)(2,1)S(1)} %shard_map.136.own), channel_id=1, source_target_pairs={{0,16},{1,17},{2,18},{3,19},{4,20},{5,21},{6,22},{7,23},{8,24},{9,... | collective-permute-start | bytes 368648 | tf_op jit(solution)/shard_map/ppermute | solution.py:320
  8.6 9.8 %collective-permute-start.2 = (bf16[96,640]{1,0:T(8,128)(2,1)S(1)}, bf16[96,640]{1,0:T(8,128)(2,1)S(1)}, u32[]{:S(2)}, u32[]{:S(2)}) collective-permute-start(bf16[96,640]{1,0:T(8,128)(2,1)S(1)} %shard_map.136.own), channel_id=1, source_target_pairs={{0,24},{1,25},{2,26},{3,27},{4,28},{5,29},{6,30},{7,31},{8,16},{9,... | collective-permute-start | bytes 368648 | tf_op jit(solution)/shard_map/ppermute | solution.py:320
  18.5 10.6 %collective-permute-start.6 = (bf16[176,640]{1,0:T(8,128)(2,1)S(1)}, bf16[176,640]{1,0:T(8,128)(2,1)S(1)}, u32[]{:S(2)}, u32[]{:S(2)}) collective-permute-start(bf16[176,640]{1,0:T(8,128)(2,1)S(1)} %get-tuple-element.37.first.wb), channel_id=1, source_target_pairs={{0,4},{1,5},{2,6},{3,7},{4,0},{5,1},{6,2},{7,3},{8,12},{9,13},{10,... | collective-permute-start | bytes 675848 | tf_op jit(solution)/shard_map/ppermute | solution.py:320
  22.6 5.9 %collective-permute-start.8 = (bf16[160,640]{1,0:T(8,128)(2,1)S(1)}, bf16[160,640]{1,0:T(8,128)(2,1)S(1)}, u32[]{:S(2)}, u32[]{:S(2)}) collective-permute-start(bf16[160,640]{1,0:T(8,128)(2,1)S(1)} %shard_map.141.first.wa), channel_id=1, source_target_pairs={{0,2},{1,3},{2,0},{3,1},{4,6},{5,7},{6,4},{7,5},{8,10},{9,11},{10,... | collective-permute-start | bytes 614408 | tf_op jit(solution)/shard_map/ppermute | solution.py:320
  28.5 11.3 %collective-permute-start.9 = (bf16[320,640]{1,0:T(8,128)(2,1)S(1)}, bf16[320,640]{1,0:T(8,128)(2,1)S(1)}, u32[]{:S(2)}, u32[]{:S(2)}) collective-permute-start(bf16[320,640]{1,0:T(8,128)(2,1)S(1)} %shard_map.142), channel_id=1, source_target_pairs={{0,4},{1,5},{2,6},{3,7},{4,0},{5,1},{6,2},{7,3},{8,12},{9,13},{10,... | collective-permute-start | bytes 1228808 | tf_op jit(solution)/shard_map/ppermute | solution.py:320
  29.0 10.8 %collective-permute-start.10 = (bf16[320,640]{1,0:T(8,128)(2,1)S(1)}, bf16[320,640]{1,0:T(8,128)(2,1)S(1)}, u32[]{:S(2)}, u32[]{:S(2)}) collective-permute-start(bf16[320,640]{1,0:T(8,128)(2,1)S(1)} %shard_map.143), channel_id=1, source_target_pairs={{0,2},{1,3},{2,0},{3,1},{4,6},{5,7},{6,4},{7,5},{8,10},{9,11},{10,... | collective-permute-start | bytes 1228808 | tf_op jit(solution)/shard_map/ppermute | solution.py:320
  30.7 7.1 %collective-permute-start.5 = (bf16[16,640]{1,0:T(8,128)(2,1)S(1)}, bf16[16,640]{1,0:T(8,128)(2,1)S(1)}, u32[]{:S(2)}, u32[]{:S(2)}) collective-permute-start(bf16[16,640]{1,0:T(8,128)(2,1)S(1)} %get-tuple-element.36.t0), channel_id=1, source_target_pairs={{0,2},{1,3},{2,0},{3,1},{4,6},{5,7},{6,4},{7,5},{8,10},{9,11},{10,... | collective-permute-start | bytes 61448 | tf_op jit(solution)/shard_map/ppermute | solution.py:320
  31.3 7.3 %collective-permute-start.7 = (bf16[16,640]{1,0:T(8,128)(2,1)S(1)}, bf16[16,640]{1,0:T(8,128)(2,1)S(1)}, u32[]{:S(2)}, u32[]{:S(2)}) collective-permute-start(bf16[16,640]{1,0:T(8,128)(2,1)S(1)} %get-tuple-element.36.t0), channel_id=1, source_target_pairs={{0,6},{1,7},{2,4},{3,5},{4,2},{5,3},{6,0},{7,1},{8,14},{9,15},{10,... | collective-permute-start | bytes 61448 | tf_op jit(solution)/shard_map/ppermute | solution.py:320
  43.5 10.2 %collective-permute-start.11 = (bf16[336,640]{1,0:T(8,128)(2,1)S(1)}, bf16[336,640]{1,0:T(8,128)(2,1)S(1)}, u32[]{:S(2)}, u32[]{:S(2)}) collective-permute-start(bf16[336,640]{1,0:T(8,128)(2,1)S(1)} %get-tuple-element.45), channel_id=1, source_target_pairs={{0,2},{1,3},{2,0},{3,1},{4,6},{5,7},{6,4},{7,5},{8,10},{9,11},{10,... | collective-permute-start | bytes 1290248 | tf_op jit(solution)/shard_map/ppermute | solution.py:320
  45.0 10.2 %collective-permute-start.14 = (bf16[320,640]{1,0:T(8,128)(2,1)S(1)}, bf16[320,640]{1,0:T(8,128)(2,1)S(1)}, u32[]{:S(2)}, u32[]{:S(2)}) collective-permute-start(bf16[320,640]{1,0:T(8,128)(2,1)S(1)} %get-tuple-element.53), channel_id=1, source_target_pairs={{0,4},{1,5},{2,6},{3,7},{4,0},{5,1},{6,2},{7,3},{8,12},{9,13},{10,... | collective-permute-start | bytes 1228808 | tf_op jit(solution)/shard_map/ppermute | solution.py:320
  53.8 6.0 %collective-permute-start.12 = (bf16[176,640]{1,0:T(8,128)(2,1)S(1)}, bf16[176,640]{1,0:T(8,128)(2,1)S(1)}, u32[]{:S(2)}, u32[]{:S(2)}) collective-permute-start(bf16[176,640]{1,0:T(8,128)(2,1)S(1)} %get-tuple-element.48), channel_id=1, source_target_pairs={{0,4},{1,5},{2,6},{3,7},{4,0},{5,1},{6,2},{7,3},{8,12},{9,13},{10,... | collective-permute-start | bytes 675848 | tf_op jit(solution)/shard_map/ppermute | solution.py:320
  55.3 19.5 %copy-start.1 = (f32[80,1280]{1,0:T(8,128)S(1)}, f32[80,1280]{1,0:T(8,128)}, u32[]{:S(2)}) copy-start(f32[80,1280]{1,0:T(8,128)} %w.1) | copy-start | bytes 1228804
  55.3 19.5 %copy-start.4 = (f32[80,1280]{1,0:T(8,128)S(1)}, f32[80,1280]{1,0:T(8,128)}, u32[]{:S(2)}) copy-start(f32[80,1280]{1,0:T(8,128)} %wm.1) | copy-start | bytes 1228804
  55.3 19.4 %copy-start.5 = (f32[80,1280]{1,0:T(8,128)S(1)}, f32[80,1280]{1,0:T(8,128)}, u32[]{:S(2)}) copy-start(f32[80,1280]{1,0:T(8,128)} %ws.1) | copy-start | bytes 1228804
  55.3 19.4 %copy-start.7 = (f32[80]{0:T(128)S(1)}, f32[80]{0:T(128)}, u32[]{:S(2)}) copy-start(f32[80]{0:T(128)} %param.13) | copy-start | bytes 964
  55.3 19.4 %copy-start.8 = (f32[80]{0:T(128)S(1)}, f32[80]{0:T(128)}, u32[]{:S(2)}) copy-start(f32[80]{0:T(128)} %param.16) | copy-start | bytes 964
  55.4 5.8 %collective-permute-start.15 = (bf16[160,640]{1,0:T(8,128)(2,1)S(1)}, bf16[160,640]{1,0:T(8,128)(2,1)S(1)}, u32[]{:S(2)}, u32[]{:S(2)}) collective-permute-start(bf16[160,640]{1,0:T(8,128)(2,1)S(1)} %get-tuple-element.55), channel_id=1, source_target_pairs={{0,2},{1,3},{2,0},{3,1},{4,6},{5,7},{6,4},{7,5},{8,10},{9,11},{10,... | collective-permute-start | bytes 614408 | tf_op jit(solution)/shard_map/ppermute | solution.py:320
  61.2 7.3 %collective-permute-start.16 = (bf16[96,640]{1,0:T(8,128)(2,1)S(1)}, bf16[96,640]{1,0:T(8,128)(2,1)S(1)}, u32[]{:S(2)}, u32[]{:S(2)}) collective-permute-start(bf16[96,640]{1,0:T(8,128)(2,1)S(1)} %get-tuple-element.56), channel_id=1, source_target_pairs={{0,16},{1,17},{2,18},{3,19},{4,20},{5,21},{6,22},{7,23},{8,24},{9,... | collective-permute-start | bytes 368648 | tf_op jit(solution)/shard_map/ppermute | solution.py:320
  65.6 6.8 %collective-permute-start.17 = (bf16[96,640]{1,0:T(8,128)(2,1)S(1)}, bf16[96,640]{1,0:T(8,128)(2,1)S(1)}, u32[]{:S(2)}, u32[]{:S(2)}) collective-permute-start(bf16[96,640]{1,0:T(8,128)(2,1)S(1)} %get-tuple-element.57), channel_id=1, source_target_pairs={{0,24},{1,25},{2,26},{3,27},{4,28},{5,29},{6,30},{7,31},{8,16},{9,... | collective-permute-start | bytes 368648 | tf_op jit(solution)/shard_map/ppermute | solution.py:320
  66.9 6.2 %collective-permute-start.13 = (bf16[96,640]{1,0:T(8,128)(2,1)S(1)}, bf16[96,640]{1,0:T(8,128)(2,1)S(1)}, u32[]{:S(2)}, u32[]{:S(2)}) collective-permute-start(bf16[96,640]{1,0:T(8,128)(2,1)S(1)} %get-tuple-element.51), channel_id=1, source_target_pairs={{0,8},{1,9},{2,10},{3,11},{4,12},{5,13},{6,14},{7,15},{8,0},{9,1},... | collective-permute-start | bytes 368648 | tf_op jit(solution)/shard_map/ppermute | solution.py:320
  73.2 1.5 %collective-permute-start.18 = (f32[88,640]{1,0:T(8,128)S(1)}, f32[88,640]{1,0:T(8,128)S(1)}, u32[]{:S(2)}, u32[]{:S(2)}) collective-permute-start(f32[88,640]{1,0:T(8,128)S(1)} %shard_map.149.mine), channel_id=1, source_target_pairs={{0,1},{1,0},{2,3},{3,2},{4,5},{5,4},{6,7},{7,6},{8,9},{9,8},{10,11... | collective-permute-start | bytes 675848 | tf_op jit(solution)/shard_map/ppermute | solution.py:324
  (5 other events, 55.3 us)

commit v3 on v2

--- a/solution.py
+++ b/solution.py
@@ -82,6 +82,7 @@
 
 VMEM = pl.BlockSpec(memory_space=pltpu.VMEM)
 ANY = pl.BlockSpec(memory_space=pl.ANY)
+HBM = pl.BlockSpec(memory_space=pltpu.HBM)
 SMEM = pl.BlockSpec(memory_space=pltpu.SMEM)
 
 
@@ -114,52 +115,31 @@
     out_ref[:unit, :] = part_ref[...].astype(BF)
 
 
-def norm_kernel(coef_ref, l_ref, n_ref, normed_ref, diff_ref):
-    rows, width = normed_ref.shape
-    half = width // 2
-    col = pl.ds(pl.multiple_of(lax.axis_index("replica") * half, 128), half)
-    a, b = coef_ref[0], coef_ref[1]
-    tile = 32
-
-    def step(i, carry):
-        at = pl.ds(pl.multiple_of(i * tile, tile), tile)
-        noisy = a * l_ref[at, :].astype(F32) + b * n_ref[at, :].astype(F32)
-        mean = jnp.sum(noisy, axis=1, keepdims=True) * (1.0 / width)
-        cent = noisy - mean
-        var = jnp.sum(cent * cent, axis=1, keepdims=True) * (1.0 / width)
-        normed_ref[at, :] = cent * (1.0 / jnp.sqrt(var + 1e-05))
-        nh = n_ref[at, col].astype(F32)
-        diff_ref[at, :] = (a * l_ref[at, col].astype(F32) + b * nh) - nh
-        return carry
-
-    lax.fori_loop(0, rows // tile, step, 0)
-
-
-def join_kernel(unit, own, z1, after, wa):
-    wa[:unit, :] = own[:unit, :]
-    wa[unit:, :] = z1[:unit, :]
-
-
-def join_gain_kernel(unit, own, z1, z2, z3, after, wb, tile):
-    for i, z in enumerate((z2, z3)):
-        wb[i * unit : (i + 1) * unit, :] = z[:unit, :]
+def join_kernel(unit, own, z1, z2, z3, wa, wb, tile):
     tile[...] = jnp.zeros_like(tile)
     for i, z in enumerate((own, z1, z2, z3)):
+        to = wa if i < 2 else wb
+        to[(i % 2) * unit : (i % 2 + 1) * unit, :] = z[:unit, :]
         tile[:, 128 * i : 128 * i + 128] = z[unit:, :128]
+    wa[2 * unit :, :] = tile[...]
     wb[2 * unit :, :] = tile[...]
 
 
-def pair_kernel(first, second, out):
+def pair_kernel(first, second, after, out):
     n = out.shape[0] // 2
     out[:n, :] = first[:n, :]
     out[n:, :] = second[:n, :]
 
 
-def act_kernel(unit, embed_ref, t0, t1, t2, t3, normed0, normed1, act_ref, slope_ref, slots, gain_ref):
+def act_kernel(
+    unit, coef_ref, embed_ref, t0, t1, t2, t3, l0, n0, l1, n1, after_a, after_b,
+    act_ref, slope_ref, diff_ref, slots, gain_ref,
+):
     me = lax.axis_index("shard")
-    both, width = act_ref.shape
-    for kp, t in enumerate((t0, t1, t2, t3)):
-        x = t[...].astype(F32)
+    width = act_ref.shape[1]
+    half = width // 2
+    for kp, (t, first) in enumerate(((t0, 0), (t1, 2 * unit), (t2, 2 * unit), (t3, 0))):
+        x = t[first : first + 16, :].astype(F32)
         line = x[0:1, :] + x[1:2, :] + x[2:3, :]
         for kz in range(4):
             slots[4 * kz + kp : 4 * kz + kp + 1, :] = line[:, 128 * kz : 128 * kz + 128]
@@ -167,14 +147,22 @@
         gain_ref[:, i * unit : (i + 1) * unit] = slots[pl.ds(me ^ i, 1), :unit]
     gain = gain_ref[...]
     embed = embed_ref[...]
+    col = pl.ds(pl.multiple_of(lax.axis_index("replica") * half, 128), half)
+    a, b = coef_ref[0], coef_ref[1]
     tile = 32
-
-    for part, normed_ref in enumerate((normed0, normed1)):
-
-        def step(i, carry, normed_ref=normed_ref, base=part * normed0.shape[0]):
+    for part, (l_ref, n_ref) in enumerate(((l0, n0), (l1, n1))):
+        rows = l_ref.shape[0]
+
+        def step(i, carry, l_ref=l_ref, n_ref=n_ref, base=part * rows):
             at = pl.ds(pl.multiple_of(i * tile, tile), tile)
             to = pl.ds(pl.multiple_of(base + i * tile, tile), tile)
-            normed = normed_ref[at, :]
+            noisy = a * l_ref[at, :].astype(F32) + b * n_ref[at, :].astype(F32)
+            mean = jnp.sum(noisy, axis=1, keepdims=True) * (1.0 / width)
+            cent = noisy - mean
+            var = jnp.sum(cent * cent, axis=1, keepdims=True) * (1.0 / width)
+            normed = cent * (1.0 / jnp.sqrt(var + 1e-05))
+            nh = n_ref[at, col].astype(F32)
+            diff_ref[to, :] = (a * l_ref[at, col].astype(F32) + b * nh) - nh
             hidden = normed * gain + embed
             sig = 0.5 * jnp.tanh(0.5 * hidden) + 0.5
             act = hidden * sig
@@ -182,11 +170,11 @@
             slope_ref[to, :] = (sig + act * (1.0 - sig)) * normed
             return carry
 
-        lax.fori_loop(0, normed_ref.shape[0] // tile, step, 0)
+        lax.fori_loop(0, rows // tile, step, 0)
 
 
 def mix_kernel(
-    scale, unit, act_ref, slope_ref, diff0, diff1, wa, wa1, wa2, wb, wb1, wb2,
+    scale, unit, act_ref, slope_ref, diff_ref, wa, wa1, wa2, wb, wb1, wb2,
     send_a, send_b, keep_a, keep_b, keep_g, w_ref, wg_ref, gout_ref, slots,
 ):
     me = lax.axis_index("shard")
@@ -207,9 +195,7 @@
         w_ref[place(2 + k, 1), :] = wb2[rows(k), :]
         w_ref[place(2 + k, 3), :] = wb2[rows(2 + k), :]
     product = jnp.dot(act_ref[...], w_ref[...], preferred_element_type=F32)
-    own_rows = diff0.shape[0]
-    gout_ref[:own_rows, :] = ((diff0[...] + product[:own_rows]) * scale).astype(BF)
-    gout_ref[own_rows:, :] = ((diff1[...] + product[own_rows:]) * scale).astype(BF)
+    gout_ref[...] = ((diff_ref[...] + product) * scale).astype(BF)
     grad_act = lax.dot_general(
         gout_ref[...], w_ref[...], (((1,), (1,)), ((), ())), preferred_element_type=F32
     )
@@ -340,11 +326,22 @@
     own = call(
         pack_kernel,
         arr((unit + 16, half), BF),
-        [ANY, VMEM],
+        [HBM, VMEM],
         [pltpu.VMEM((unit, half), F32), pltpu.SemaphoreType.DMA],
         byts=6 * unit * half,
     )(master_weight, norm_gain.reshape(1, unit))
     z1, z2, z3 = to(own, 4), to(own, 8), to(own, 12)
+    wa, wb, tile = call(
+        functools.partial(join_kernel, unit),
+        (arr((two + 16, half), BF), arr((two + 16, half), BF), arr((16, half), BF)),
+        [VMEM] * 4,
+        byts=16 * unit * half,
+    )(own, z1, z2, z3)
+    wa1, wb1 = to(wa, 1), to(wb, 2)
+    far = to(tile, 3)
+    pair = call(pair_kernel, arr((four, half), BF), [VMEM] * 2 + [ANY], byts=16 * unit * half)
+    pair_a, pair_b = pair(wa, wa1, far), pair(wb, wb1, far)
+    wa2, wb2 = to(pair_a, 2), to(pair_b, 1)
 
     other_latents, other_noise = across(latents), across(noise)
     step_time = lax.dynamic_slice(timesteps, (me * cores * rows // VOX,), (1,)).astype(F32)
@@ -352,43 +349,13 @@
     coef = jnp.concatenate([jnp.sqrt(level), jnp.sqrt(1.0 - level)])
     angles = step_time[:, None] * frequencies(width)[None, :]
     embed = jnp.concatenate([jnp.sin(angles), jnp.cos(angles)], axis=1)
-    normalize = call(
-        norm_kernel,
-        (arr((rows, width), F32), arr((rows, half), F32)),
-        [SMEM] + [VMEM] * 2,
-        flops=10 * rows * width,
-        byts=8 * rows * width,
-    )
-    normed0, diff0 = normalize(coef, latents, noise)
-    normed1, diff1 = normalize(coef, other_latents, other_noise)
-
-    wa = call(
-        functools.partial(join_kernel, unit),
-        arr((two, half), BF),
-        [VMEM] * 2 + [ANY],
-        byts=8 * unit * half,
-    )(own, z1, diff0)
-    wa1 = to(wa, 1)
-    wb, gain_tile = call(
-        functools.partial(join_gain_kernel, unit),
-        (arr((two + 16, half), BF), arr((16, half), BF)),
-        [VMEM] * 4 + [ANY],
-        byts=8 * unit * half,
-    )(own, z1, z2, z3, diff1)
-    wb1 = to(wb, 2)
-    gain_x, gain_xy = to(gain_tile, 1), to(gain_tile, 3)
-    pair = call(pair_kernel, arr((four, half), BF), [VMEM] * 2, byts=16 * unit * half)
-    wa2 = to(pair(wa, wa1), 2)
-    wb2 = to(pair(wb, wb1), 1)
-    gain_y = wb1[two:]
-    act, slope = call(
+    act, slope, diff = call(
         functools.partial(act_kernel, unit),
-        (arr((both, width), BF), arr((both, width), F32)),
-        [VMEM] * 7,
+        (arr((both, width), BF), arr((both, width), F32), arr((both, half), F32)),
+        [SMEM] + [VMEM] * 9 + [ANY] * 2,
         [pltpu.VMEM((16, 128), F32), pltpu.VMEM((1, width), F32)],
-        flops=20 * both * width,
-        byts=8 * both * width,
-    )(embed, gain_tile, gain_x, gain_y, gain_xy, normed0, normed1)
+        byts=28 * both * width,
+    )(coef, embed, tile, wa1, wb1, far, latents, noise, other_latents, other_noise, pair_a, pair_b)
 
     send_a, send_b, keep_a, keep_b, keep_g = call(
         functools.partial(mix_kernel, 1.0 / math.sqrt(total_rows), unit),
@@ -399,7 +366,7 @@
             arr((four, half), F32),
             arr((8, half), F32),
         ),
-        [VMEM] * 10,
+        [VMEM] * 9,
         [
             pltpu.VMEM((width, half), BF),
             pltpu.VMEM((width, half), F32),
@@ -408,7 +375,7 @@
         ],
         flops=6 * both * width * half,
         byts=6 * both * width,
-    )(act, slope, diff0, diff1, wa, wa1, wa2, wb, wb1, wb2)
+    )(act, slope, diff, wa, wa1, wa2, wb, wb1, wb2)
 
     got_a, got_b = to(send_a, 1), to(send_b, 2)
     send_a, own_a, own_g = call(

time: 76.3 us -> 70.7 us (0.927)
  starting transfers between devices: 24.8 us -> 19.5 us
    ppermute x16 -> x15, starting transfers between devices: 24.1 us -> 19 us  [to(): return lax.ppermute(x, AXES, pairs)]
    pallas_call x7 -> x4, Pallas kernels: 5.15 us -> 0.76 us  [the longest x1 0.64 us: paired_body(): call(functools.partial(join_kernel, unit), (arr((two + 16, half), BF), ar...]
    pallas_call x1, Pallas kernels: 1.22 us -> 5.38 us  [paired_body(): call(functools.partial(act_kernel, unit), (arr((both, width), BF), arr((b...]
    ppermute x16 -> x15, waiting for transfers between devices: 33.3 us -> 33.3 us  [to(): return lax.ppermute(x, AXES, pairs)]
  transfers between devices with their start and end apart: 19 -> 18, of which waited for: 12 -> 11; matrix products, arithmetic and copies ran while one was open for 2% -> 2% of each run, Pallas kernels for 9% -> 8%
where the time goes in v3:
time: 70.7 us; the launch traced here: 70.5 us
  waiting for transfers between devices  34.7 us (49%)
  starting transfers between devices  19.5 us (28%)
  Pallas kernels  11.4 us (16%)
  local copies, waits for them, and re-layouts  2.93 us (4%)
  between operations  1.66 us (2%)
    ppermute x15, waiting for transfers between devices, to(): return lax.ppermute(x, AXES, pairs)  33.3 us
    ppermute x15, starting transfers between devices, to(): return lax.ppermute(x, AXES, pairs)  19 us
    pallas_call x1, Pallas kernels, paired_body(): call(functools.partial(act_kernel, unit), (arr((both, width), BF), arr((b...  5.38 us
    pallas_call x1, Pallas kernels, paired_body(): call(functools.partial(mix_kernel, 1.0 / math.sqrt(total_rows), unit), (a...  3.61 us
    unnamed x20, local copies, waits for them, and re-layouts  1.7 us
    ppermute x3, waiting for transfers between devices, across(): return lax.ppermute(x, AXES, pairs)  1.47 us
  transfers between devices with their start and end apart: 18, of which 11 were waited for; matrix products, arithmetic and copies ran while one was open for 2% of the time, Pallas kernels for 8%

profile of v3, /device:TPU:0, one launch (start us, length us, event | category | flops | bytes accessed | tf_op | source)
XLA Modules:
  0.0 70.5 jit_solution(4617152957414461984)
XLA Ops:
  0.6 1.0 %copy-done = f32[80,1280]{1,0:T(8,128)S(1)} copy-done((f32[80,1280]{1,0:T(8,128)S(1)}, f32[80,1280]{1,0:T(8,128)}, u32[]{:S(2)}) %copy-start) | copy-done | bytes 409624
  2.4 5.1 %collective-permute-start.2 = (bf16[96,640]{1,0:T(8,128)(2,1)S(1)}, bf16[96,640]{1,0:T(8,128)(2,1)S(1)}, u32[]{:S(2)}, u32[]{:S(2)}) collective-permute-start(bf16[96,640]{1,0:T(8,128)(2,1)S(1)} %shard_map.136.own), channel_id=1, source_target_pairs={{0,24},{1,25},{2,26},{3,27},{4,28},{5,29},{6,30},{7,31},{8,16},{9,... | collective-permute-start | bytes 368648 | tf_op jit(solution)/shard_map/ppermute | solution.py:306
  8.1 3.6 %collective-permute-done.2.z3 = bf16[96,640]{1,0:T(8,128)(2,1)S(1)} collective-permute-done((bf16[96,640]{1,0:T(8,128)(2,1)S(1)}, bf16[96,640]{1,0:T(8,128)(2,1)S(1)}, u32[]{:S(2)}, u32[]{:S(2)}) %collective-permute-start.2) | collective-permute-done | bytes 122912 | tf_op jit(solution)/shard_map/ppermute | solution.py:306
  11.7 6.1 %collective-permute-done.1.z2 = bf16[96,640]{1,0:T(8,128)(2,1)S(1)} collective-permute-done((bf16[96,640]{1,0:T(8,128)(2,1)S(1)}, bf16[96,640]{1,0:T(8,128)(2,1)S(1)}, u32[]{:S(2)}, u32[]{:S(2)}) %collective-permute-start.1) | collective-permute-done | bytes 122912 | tf_op jit(solution)/shard_map/ppermute | solution.py:306
  18.5 1.5 %collective-permute-start.3 = (bf16[176,640]{1,0:T(8,128)(2,1)S(1)}, bf16[176,640]{1,0:T(8,128)(2,1)S(1)}, u32[]{:S(2)}, u32[]{:S(2)}) collective-permute-start(bf16[176,640]{1,0:T(8,128)(2,1)S(1)} %get-tuple-element.34.first.wa), channel_id=1, source_target_pairs={{0,2},{1,3},{2,0},{3,1},{4,6},{5,7},{6,4},{7,5},{8,10},{9,11},{10,... | collective-permute-start | bytes 675848 | tf_op jit(solution)/shard_map/ppermute | solution.py:306
  20.0 1.5 %collective-permute-start.4 = (bf16[176,640]{1,0:T(8,128)(2,1)S(1)}, bf16[176,640]{1,0:T(8,128)(2,1)S(1)}, u32[]{:S(2)}, u32[]{:S(2)}) collective-permute-start(bf16[176,640]{1,0:T(8,128)(2,1)S(1)} %get-tuple-element.35.first.wb), channel_id=1, source_target_pairs={{0,4},{1,5},{2,6},{3,7},{4,0},{5,1},{6,2},{7,3},{8,12},{9,13},{10,... | collective-permute-start | bytes 675848 | tf_op jit(solution)/shard_map/ppermute | solution.py:306
  22.5 1.2 %dynamic_slice.3 = s32[1]{0:T(128)} dynamic-slice(s32[16]{0:T(128)} %param.11, s32[]{:T(128)S(6)} %select_n.9), dynamic_slice_sizes={1} | dynamic-slice | bytes 12 | tf_op jit(solution)/shard_map/dynamic_slice | solution.py:347
  24.5 2.4 %collective-permute-done.5.after.t3 = bf16[16,640]{1,0:T(8,128)(2,1)S(1)} collective-permute-done((bf16[16,640]{1,0:T(8,128)(2,1)}, bf16[16,640]{1,0:T(8,128)(2,1)S(1)}, u32[]{:S(2)}, u32[]{:S(2)}) %collective-permute-start.5) | collective-permute-done | bytes 20512 | tf_op jit(solution)/shard_map/ppermute | solution.py:306
  27.7 1.1 %collective-permute-start.9 = (bf16[320,640]{1,0:T(8,128)(2,1)S(1)}, bf16[320,640]{1,0:T(8,128)(2,1)S(1)}, u32[]{:S(2)}, u32[]{:S(2)}) collective-permute-start(bf16[320,640]{1,0:T(8,128)(2,1)S(1)} %shard_map.139.after_b), channel_id=1, source_target_pairs={{0,2},{1,3},{2,0},{3,1},{4,6},{5,7},{6,4},{7,5},{8,10},{9,11},{10,... | collective-permute-start | bytes 1228808 | tf_op jit(solution)/shard_map/ppermute | solution.py:306
  29.0 5.4 %shard_map.140 = (bf16[512,1280]{1,0:T(8,128)(2,1)S(1)}, f32[512,1280]{1,0:T(8,128)S(1)}, f32[512,640]{1,0:T(8,128)S(1)}) custom-call(f32[2]{0:T(128)S(1)} %pad_maximum_fusion.1.coef_ref, f32[1,1280]{1,0:T(1,128)S(1)} %pad_maximum_fusion.embed_ref, bf16[16,640]{1,0:T(8,128)(2,1)} %get-tuple-element.33.t0, ...), custom_call_target="tpu_custom_call" | custom-call | bytes 18350080 | tf_op jit(solution)/shard_map/pallas_call | solution.py:352
  34.4 3.1 %collective-permute-done.8.wa2 = bf16[320,640]{1,0:T(8,128)(2,1)S(1)} collective-permute-done((bf16[320,640]{1,0:T(8,128)(2,1)S(1)}, bf16[320,640]{1,0:T(8,128)(2,1)S(1)}, u32[]{:S(2)}, u32[]{:S(2)}) %collective-permute-start.8) | collective-permute-done | bytes 409632 | tf_op jit(solution)/shard_map/ppermute | solution.py:306
  37.9 3.6 %shard_map.141 = (bf16[336,640]{1,0:T(8,128)(2,1)S(1)}, bf16[320,640]{1,0:T(8,128)(2,1)S(1)}, f32[320,640]{1,0:T(8,128)S(1)}, f32[320,640]{1,0:T(8,128)S(1)}, f32[8,640]{1,0:T(8,128)S(1)}) custom-call(bf16[512,1280]{1,0:T(8,128)(2,1)S(1)} %get-tuple-element.36.act_ref, f32[512,1280]{1,0:T(8,128)S(1)} %get-tuple-element.37.slope_ref, ...), custom_call_target="tpu_custom_call" | custom-call | flops 2516582400 | bytes 3932160 | tf_op jit(solution)/shard_map/pallas_call | solution.py:360
  42.3 1.3 %collective-permute-start.13 = (bf16[320,640]{1,0:T(8,128)(2,1)S(1)}, bf16[320,640]{1,0:T(8,128)(2,1)S(1)}, u32[]{:S(2)}, u32[]{:S(2)}) collective-permute-start(bf16[320,640]{1,0:T(8,128)(2,1)S(1)} %get-tuple-element.49), channel_id=1, source_target_pairs={{0,4},{1,5},{2,6},{3,7},{4,0},{5,1},{6,2},{7,3},{8,12},{9,13},{10,... | collective-permute-start | bytes 1228808 | tf_op jit(solution)/shard_map/ppermute | solution.py:306
  43.6 7.6 %collective-permute-done.10.got = bf16[336,640]{1,0:T(8,128)(2,1)S(1)} collective-permute-done((bf16[336,640]{1,0:T(8,128)(2,1)S(1)}, bf16[336,640]{1,0:T(8,128)(2,1)S(1)}, u32[]{:S(2)}, u32[]{:S(2)}) %collective-permute-start.10) | collective-permute-done | bytes 430112 | tf_op jit(solution)/shard_map/ppermute | solution.py:306
  51.3 1.6 %collective-permute-start.11 = (bf16[176,640]{1,0:T(8,128)(2,1)S(1)}, bf16[176,640]{1,0:T(8,128)(2,1)S(1)}, u32[]{:S(2)}, u32[]{:S(2)}) collective-permute-start(bf16[176,640]{1,0:T(8,128)(2,1)S(1)} %get-tuple-element.44), channel_id=1, source_target_pairs={{0,4},{1,5},{2,6},{3,7},{4,0},{5,1},{6,2},{7,3},{8,12},{9,13},{10,... | collective-permute-start | bytes 675848 | tf_op jit(solution)/shard_map/ppermute | solution.py:306
  53.1 1.1 %collective-permute-start.14 = (bf16[160,640]{1,0:T(8,128)(2,1)S(1)}, bf16[160,640]{1,0:T(8,128)(2,1)S(1)}, u32[]{:S(2)}, u32[]{:S(2)}) collective-permute-start(bf16[160,640]{1,0:T(8,128)(2,1)S(1)} %get-tuple-element.51), channel_id=1, source_target_pairs={{0,2},{1,3},{2,0},{3,1},{4,6},{5,7},{6,4},{7,5},{8,10},{9,11},{10,... | collective-permute-start | bytes 614408 | tf_op jit(solution)/shard_map/ppermute | solution.py:306
  54.2 3.2 %collective-permute-done.11.got = bf16[176,640]{1,0:T(8,128)(2,1)S(1)} collective-permute-done((bf16[176,640]{1,0:T(8,128)(2,1)S(1)}, bf16[176,640]{1,0:T(8,128)(2,1)S(1)}, u32[]{:S(2)}, u32[]{:S(2)}) %collective-permute-start.11) | collective-permute-done | bytes 225312 | tf_op jit(solution)/shard_map/ppermute | solution.py:306
  57.5 1.4 %collective-permute-done.14.got = bf16[160,640]{1,0:T(8,128)(2,1)S(1)} collective-permute-done((bf16[160,640]{1,0:T(8,128)(2,1)S(1)}, bf16[160,640]{1,0:T(8,128)(2,1)S(1)}, u32[]{:S(2)}, u32[]{:S(2)}) %collective-permute-start.14) | collective-permute-done | bytes 204832 | tf_op jit(solution)/shard_map/ppermute | solution.py:306
  59.0 1.5 %collective-permute-start.15 = (bf16[96,640]{1,0:T(8,128)(2,1)S(1)}, bf16[96,640]{1,0:T(8,128)(2,1)S(1)}, u32[]{:S(2)}, u32[]{:S(2)}) collective-permute-start(bf16[96,640]{1,0:T(8,128)(2,1)S(1)} %get-tuple-element.52), channel_id=1, source_target_pairs={{0,16},{1,17},{2,18},{3,19},{4,20},{5,21},{6,22},{7,23},{8,24},{9,... | collective-permute-start | bytes 368648 | tf_op jit(solution)/shard_map/ppermute | solution.py:306
  60.5 1.5 %collective-permute-start.16 = (bf16[96,640]{1,0:T(8,128)(2,1)S(1)}, bf16[96,640]{1,0:T(8,128)(2,1)S(1)}, u32[]{:S(2)}, u32[]{:S(2)}) collective-permute-start(bf16[96,640]{1,0:T(8,128)(2,1)S(1)} %get-tuple-element.53), channel_id=1, source_target_pairs={{0,24},{1,25},{2,26},{3,27},{4,28},{5,29},{6,30},{7,31},{8,16},{9,... | collective-permute-start | bytes 368648 | tf_op jit(solution)/shard_map/ppermute | solution.py:306
  62.0 1.4 %collective-permute-done.12.h1 = bf16[96,640]{1,0:T(8,128)(2,1)S(1)} collective-permute-done((bf16[96,640]{1,0:T(8,128)(2,1)S(1)}, bf16[96,640]{1,0:T(8,128)(2,1)S(1)}, u32[]{:S(2)}, u32[]{:S(2)}) %collective-permute-start.12) | collective-permute-done | bytes 122912 | tf_op jit(solution)/shard_map/ppermute | solution.py:306
  63.4 4.1 %collective-permute-done.15.h2 = bf16[96,640]{1,0:T(8,128)(2,1)S(1)} collective-permute-done((bf16[96,640]{1,0:T(8,128)(2,1)S(1)}, bf16[96,640]{1,0:T(8,128)(2,1)S(1)}, u32[]{:S(2)}, u32[]{:S(2)}) %collective-permute-start.15) | collective-permute-done | bytes 122912 | tf_op jit(solution)/shard_map/ppermute | solution.py:306
  67.6 1.5 %collective-permute-done.17.theirs = f32[88,640]{1,0:T(8,128)S(1)} collective-permute-done((f32[88,640]{1,0:T(8,128)S(1)}, f32[88,640]{1,0:T(8,128)S(1)}, u32[]{:S(2)}, u32[]{:S(2)}) %collective-permute-start.17) | collective-permute-done | bytes 225312 | tf_op jit(solution)/shard_map/ppermute | solution.py:310
  69.1 1.3 %shard_map.147 = (f32[80,1280]{1,0:T(8,128)}, f32[80,1280]{1,0:T(8,128)}, f32[80,1280]{1,0:T(8,128)}, f32[1,80]{1,0:T(1,128)}, f32[1,80]{1,0:T(1,128)}, /*index=5*/f32[1,80]{1,0:T(1,128)}) custom-call(f32[88,640]{1,0:T(8,128)S(1)} %shard_map.146.mine, f32[88,640]{1,0:T(8,128)S(1)} %collective-permute-done.17.theirs, f32[80,1280]{1,0:T(8,128)S(1)} %copy-done.1, ...), custom_call_target="tpu_custom_call" | custom-call | bytes 2457600 | tf_op jit(solution)/shard_map/pallas_call | solution.py:418
  (48 shorter events, 5.6 us)
Async XLA Ops:
  2.3 26.7 %copy-start.2 = (bf16[256,1280]{1,0:T(8,128)(2,1)S(1)}, bf16[256,1280]{1,0:T(8,128)(2,1)}, u32[]{:S(2)}) copy-start(bf16[256,1280]{1,0:T(8,128)(2,1)} %l0.1) | copy-start | bytes 1966084
  2.3 26.7 %copy-start.3 = (bf16[256,1280]{1,0:T(8,128)(2,1)S(1)}, bf16[256,1280]{1,0:T(8,128)(2,1)}, u32[]{:S(2)}) copy-start(bf16[256,1280]{1,0:T(8,128)(2,1)} %n0.1) | copy-start | bytes 1966084
  2.4 9.4 %collective-permute-start.2 = (bf16[96,640]{1,0:T(8,128)(2,1)S(1)}, bf16[96,640]{1,0:T(8,128)(2,1)S(1)}, u32[]{:S(2)}, u32[]{:S(2)}) collective-permute-start(bf16[96,640]{1,0:T(8,128)(2,1)S(1)} %shard_map.136.own), channel_id=1, source_target_pairs={{0,24},{1,25},{2,26},{3,27},{4,28},{5,29},{6,30},{7,31},{8,16},{9,... | collective-permute-start | bytes 368648 | tf_op jit(solution)/shard_map/ppermute | solution.py:306
  7.5 10.4 %collective-permute-start.1 = (bf16[96,640]{1,0:T(8,128)(2,1)S(1)}, bf16[96,640]{1,0:T(8,128)(2,1)S(1)}, u32[]{:S(2)}, u32[]{:S(2)}) collective-permute-start(bf16[96,640]{1,0:T(8,128)(2,1)S(1)} %shard_map.136.own), channel_id=1, source_target_pairs={{0,16},{1,17},{2,18},{3,19},{4,20},{5,21},{6,22},{7,23},{8,24},{9,... | collective-permute-start | bytes 368648 | tf_op jit(solution)/shard_map/ppermute | solution.py:306
  7.5 10.4 %collective-permute-start = (bf16[96,640]{1,0:T(8,128)(2,1)S(1)}, bf16[96,640]{1,0:T(8,128)(2,1)S(1)}, u32[]{:S(2)}, u32[]{:S(2)}) collective-permute-start(bf16[96,640]{1,0:T(8,128)(2,1)S(1)} %shard_map.136.own), channel_id=1, source_target_pairs={{0,8},{1,9},{2,10},{3,11},{4,12},{5,13},{6,14},{7,15},{8,0},{9,1},... | collective-permute-start | bytes 368648 | tf_op jit(solution)/shard_map/ppermute | solution.py:306
  18.5 8.4 %collective-permute-start.3 = (bf16[176,640]{1,0:T(8,128)(2,1)S(1)}, bf16[176,640]{1,0:T(8,128)(2,1)S(1)}, u32[]{:S(2)}, u32[]{:S(2)}) collective-permute-start(bf16[176,640]{1,0:T(8,128)(2,1)S(1)} %get-tuple-element.34.first.wa), channel_id=1, source_target_pairs={{0,2},{1,3},{2,0},{3,1},{4,6},{5,7},{6,4},{7,5},{8,10},{9,11},{10,... | collective-permute-start | bytes 675848 | tf_op jit(solution)/shard_map/ppermute | solution.py:306
  20.0 7.6 %collective-permute-start.4 = (bf16[176,640]{1,0:T(8,128)(2,1)S(1)}, bf16[176,640]{1,0:T(8,128)(2,1)S(1)}, u32[]{:S(2)}, u32[]{:S(2)}) collective-permute-start(bf16[176,640]{1,0:T(8,128)(2,1)S(1)} %get-tuple-element.35.first.wb), channel_id=1, source_target_pairs={{0,4},{1,5},{2,6},{3,7},{4,0},{5,1},{6,2},{7,3},{8,12},{9,13},{10,... | collective-permute-start | bytes 675848 | tf_op jit(solution)/shard_map/ppermute | solution.py:306
  21.5 7.5 %collective-permute-start.6 = (bf16[256,1280]{1,0:T(8,128)(2,1)}, bf16[256,1280]{1,0:T(8,128)(2,1)S(1)}, u32[]{:S(2)}, u32[]{:S(2)}) collective-permute-start(bf16[256,1280]{1,0:T(8,128)(2,1)} %l0.1), channel_id=1, source_target_pairs={{0,1},{1,0},{2,3},{3,2},{4,5},{5,4},{6,7},{7,6},{8,9},{9,8},{10,11... | collective-permute-start | bytes 1966088 | tf_op jit(solution)/shard_map/ppermute | solution.py:310
  21.5 7.5 %collective-permute-start.7 = (bf16[256,1280]{1,0:T(8,128)(2,1)}, bf16[256,1280]{1,0:T(8,128)(2,1)S(1)}, u32[]{:S(2)}, u32[]{:S(2)}) collective-permute-start(bf16[256,1280]{1,0:T(8,128)(2,1)} %n0.1), channel_id=1, source_target_pairs={{0,1},{1,0},{2,3},{3,2},{4,5},{5,4},{6,7},{7,6},{8,9},{9,8},{10,11... | collective-permute-start | bytes 1966088 | tf_op jit(solution)/shard_map/ppermute | solution.py:310
  22.0 4.9 %collective-permute-start.5 = (bf16[16,640]{1,0:T(8,128)(2,1)}, bf16[16,640]{1,0:T(8,128)(2,1)S(1)}, u32[]{:S(2)}, u32[]{:S(2)}) collective-permute-start(bf16[16,640]{1,0:T(8,128)(2,1)} %get-tuple-element.33.t0), channel_id=1, source_target_pairs={{0,6},{1,7},{2,4},{3,5},{4,2},{5,3},{6,0},{7,1},{8,14},{9,15},{10,... | collective-permute-start | bytes 61448 | tf_op jit(solution)/shard_map/ppermute | solution.py:306
  26.9 10.6 %collective-permute-start.8 = (bf16[320,640]{1,0:T(8,128)(2,1)S(1)}, bf16[320,640]{1,0:T(8,128)(2,1)S(1)}, u32[]{:S(2)}, u32[]{:S(2)}) collective-permute-start(bf16[320,640]{1,0:T(8,128)(2,1)S(1)} %shard_map.138.after_a), channel_id=1, source_target_pairs={{0,4},{1,5},{2,6},{3,7},{4,0},{5,1},{6,2},{7,3},{8,12},{9,13},{10,... | collective-permute-start | bytes 1228808 | tf_op jit(solution)/shard_map/ppermute | solution.py:306
  27.7 10.2 %collective-permute-start.9 = (bf16[320,640]{1,0:T(8,128)(2,1)S(1)}, bf16[320,640]{1,0:T(8,128)(2,1)S(1)}, u32[]{:S(2)}, u32[]{:S(2)}) collective-permute-start(bf16[320,640]{1,0:T(8,128)(2,1)S(1)} %shard_map.139.after_b), channel_id=1, source_target_pairs={{0,2},{1,3},{2,0},{3,1},{4,6},{5,7},{6,4},{7,5},{8,10},{9,11},{10,... | collective-permute-start | bytes 1228808 | tf_op jit(solution)/shard_map/ppermute | solution.py:306
  41.5 9.8 %collective-permute-start.10 = (bf16[336,640]{1,0:T(8,128)(2,1)S(1)}, bf16[336,640]{1,0:T(8,128)(2,1)S(1)}, u32[]{:S(2)}, u32[]{:S(2)}) collective-permute-start(bf16[336,640]{1,0:T(8,128)(2,1)S(1)} %get-tuple-element.41), channel_id=1, source_target_pairs={{0,2},{1,3},{2,0},{3,1},{4,6},{5,7},{6,4},{7,5},{8,10},{9,11},{10,... | collective-permute-start | bytes 1290248 | tf_op jit(solution)/shard_map/ppermute | solution.py:306
  42.3 10.7 %collective-permute-start.13 = (bf16[320,640]{1,0:T(8,128)(2,1)S(1)}, bf16[320,640]{1,0:T(8,128)(2,1)S(1)}, u32[]{:S(2)}, u32[]{:S(2)}) collective-permute-start(bf16[320,640]{1,0:T(8,128)(2,1)S(1)} %get-tuple-element.49), channel_id=1, source_target_pairs={{0,4},{1,5},{2,6},{3,7},{4,0},{5,1},{6,2},{7,3},{8,12},{9,13},{10,... | collective-permute-start | bytes 1228808 | tf_op jit(solution)/shard_map/ppermute | solution.py:306
  51.3 6.0 %collective-permute-start.11 = (bf16[176,640]{1,0:T(8,128)(2,1)S(1)}, bf16[176,640]{1,0:T(8,128)(2,1)S(1)}, u32[]{:S(2)}, u32[]{:S(2)}) collective-permute-start(bf16[176,640]{1,0:T(8,128)(2,1)S(1)} %get-tuple-element.44), channel_id=1, source_target_pairs={{0,4},{1,5},{2,6},{3,7},{4,0},{5,1},{6,2},{7,3},{8,12},{9,13},{10,... | collective-permute-start | bytes 675848 | tf_op jit(solution)/shard_map/ppermute | solution.py:306
  53.0 16.0 %copy-start.1 = (f32[80,1280]{1,0:T(8,128)S(1)}, f32[80,1280]{1,0:T(8,128)}, u32[]{:S(2)}) copy-start(f32[80,1280]{1,0:T(8,128)} %w.1) | copy-start | bytes 1228804
  53.1 16.0 %copy-start.4 = (f32[80,1280]{1,0:T(8,128)S(1)}, f32[80,1280]{1,0:T(8,128)}, u32[]{:S(2)}) copy-start(f32[80,1280]{1,0:T(8,128)} %wm.1) | copy-start | bytes 1228804
  53.1 16.0 %copy-start.5 = (f32[80,1280]{1,0:T(8,128)S(1)}, f32[80,1280]{1,0:T(8,128)}, u32[]{:S(2)}) copy-start(f32[80,1280]{1,0:T(8,128)} %ws.1) | copy-start | bytes 1228804
  53.1 16.0 %copy-start.7 = (f32[80]{0:T(128)S(1)}, f32[80]{0:T(128)}, u32[]{:S(2)}) copy-start(f32[80]{0:T(128)} %param.13) | copy-start | bytes 964
  53.1 5.8 %collective-permute-start.14 = (bf16[160,640]{1,0:T(8,128)(2,1)S(1)}, bf16[160,640]{1,0:T(8,128)(2,1)S(1)}, u32[]{:S(2)}, u32[]{:S(2)}) collective-permute-start(bf16[160,640]{1,0:T(8,128)(2,1)S(1)} %get-tuple-element.51), channel_id=1, source_target_pairs={{0,2},{1,3},{2,0},{3,1},{4,6},{5,7},{6,4},{7,5},{8,10},{9,11},{10,... | collective-permute-start | bytes 614408 | tf_op jit(solution)/shard_map/ppermute | solution.py:306
  57.4 6.0 %collective-permute-start.12 = (bf16[96,640]{1,0:T(8,128)(2,1)S(1)}, bf16[96,640]{1,0:T(8,128)(2,1)S(1)}, u32[]{:S(2)}, u32[]{:S(2)}) collective-permute-start(bf16[96,640]{1,0:T(8,128)(2,1)S(1)} %get-tuple-element.47), channel_id=1, source_target_pairs={{0,8},{1,9},{2,10},{3,11},{4,12},{5,13},{6,14},{7,15},{8,0},{9,1},... | collective-permute-start | bytes 368648 | tf_op jit(solution)/shard_map/ppermute | solution.py:306
  59.0 8.5 %collective-permute-start.15 = (bf16[96,640]{1,0:T(8,128)(2,1)S(1)}, bf16[96,640]{1,0:T(8,128)(2,1)S(1)}, u32[]{:S(2)}, u32[]{:S(2)}) collective-permute-start(bf16[96,640]{1,0:T(8,128)(2,1)S(1)} %get-tuple-element.52), channel_id=1, source_target_pairs={{0,16},{1,17},{2,18},{3,19},{4,20},{5,21},{6,22},{7,23},{8,24},{9,... | collective-permute-start | bytes 368648 | tf_op jit(solution)/shard_map/ppermute | solution.py:306
  60.5 6.9 %collective-permute-start.16 = (bf16[96,640]{1,0:T(8,128)(2,1)S(1)}, bf16[96,640]{1,0:T(8,128)(2,1)S(1)}, u32[]{:S(2)}, u32[]{:S(2)}) collective-permute-start(bf16[96,640]{1,0:T(8,128)(2,1)S(1)} %get-tuple-element.53), channel_id=1, source_target_pairs={{0,24},{1,25},{2,26},{3,27},{4,28},{5,29},{6,30},{7,31},{8,16},{9,... | collective-permute-start | bytes 368648 | tf_op jit(solution)/shard_map/ppermute | solution.py:306
  67.5 1.5 %collective-permute-start.17 = (f32[88,640]{1,0:T(8,128)S(1)}, f32[88,640]{1,0:T(8,128)S(1)}, u32[]{:S(2)}, u32[]{:S(2)}) collective-permute-start(f32[88,640]{1,0:T(8,128)S(1)} %shard_map.146.mine), channel_id=1, source_target_pairs={{0,1},{1,0},{2,3},{3,2},{4,5},{5,4},{6,7},{7,6},{8,9},{9,8},{10,11... | collective-permute-start | bytes 675848 | tf_op jit(solution)/shard_map/ppermute | solution.py:310
  (4 other events, 33.7 us)

commit v4 on v3

--- a/solution.py
+++ b/solution.py
@@ -103,12 +103,15 @@
     return tile
 
 
-def pack_kernel(w_ref, gain_ref, out_ref, part_ref, sem):
+def pack_kernel(w_ref, gain_hbm, out_ref, part_ref, gain_ref, sem, gain_sem):
     unit, half = part_ref.shape
     col = pl.ds(pl.multiple_of(lax.axis_index("replica") * half, 128), half)
     copy = pltpu.make_async_copy(w_ref.at[:, col], part_ref, sem)
     copy.start()
+    gain_copy = pltpu.make_async_copy(gain_hbm, gain_ref, gain_sem)
+    gain_copy.start()
     out_ref[unit:, :] = jnp.zeros((16, half), BF)
+    gain_copy.wait()
     gain = stack_rows(split(gain_ref[...], 3), (16, unit))
     out_ref[unit:, :unit] = gain.astype(BF)
     copy.wait()
@@ -174,8 +177,8 @@
 
 
 def mix_kernel(
-    scale, unit, act_ref, slope_ref, diff_ref, wa, wa1, wa2, wb, wb1, wb2,
-    send_a, send_b, keep_a, keep_b, keep_g, w_ref, wg_ref, gout_ref, slots,
+    scale, unit, act_ref, diff_ref, wa, wa1, wa2, wb, wb1, wb2,
+    send_a, send_b, keep_a, keep_b, w_ref, gout_ref, wg_ref,
 ):
     me = lax.axis_index("shard")
 
@@ -196,24 +199,9 @@
         w_ref[place(2 + k, 3), :] = wb2[rows(2 + k), :]
     product = jnp.dot(act_ref[...], w_ref[...], preferred_element_type=F32)
     gout_ref[...] = ((diff_ref[...] + product) * scale).astype(BF)
-    grad_act = lax.dot_general(
-        gout_ref[...], w_ref[...], (((1,), (1,)), ((), ())), preferred_element_type=F32
-    )
-    part = jnp.sum(grad_act * slope_ref[...], axis=0, keepdims=True)
     wg_ref[...] = lax.dot_general(
         act_ref[...], gout_ref[...], (((0,), (0,)), ((), ())), preferred_element_type=F32
     )
-    half = wg_ref.shape[1]
-    slots[...] = jnp.zeros_like(slots)
-    for i in range(16):
-        slots[pl.ds(me ^ i, 1), :unit] = part[:, i * unit : (i + 1) * unit]
-    lines = [
-        jnp.concatenate([slots[4 * kz + kp : 4 * kz + kp + 1, :] for kz in range(4)], axis=1)
-        for kp in range(4)
-    ]
-    keep_g[...] = jnp.zeros_like(keep_g)
-    keep_g[0:1, :512] = lines[0]
-    keep_g[1:2, :512] = lines[2]
     for k in range(2):
         send_a[rows(k), :] = wg_ref[place(k, 1), :].astype(BF)
         send_a[rows(2 + k), :] = wg_ref[place(k, 3), :].astype(BF)
@@ -223,18 +211,28 @@
         send_b[rows(2 + k), :] = wg_ref[place(2 + k, 3), :].astype(BF)
         keep_b[rows(k), :] = wg_ref[place(2 + k, 0), :]
         keep_b[rows(2 + k), :] = wg_ref[place(2 + k, 1), :]
-    send_a[4 * unit :, :] = jnp.zeros((16, half), BF)
-    send_a[4 * unit :, :512] = stack_rows(split(lines[1], 2) + split(lines[3], 2), (16, 512)).astype(BF)
-
-
-def fold_a_kernel(unit, keep_a, keep_g, got, send, own, own_g):
+
+
+def gain_kernel(unit, gout_ref, w_ref, slope_ref, keep, send, slots):
+    me = lax.axis_index("shard")
+    grad_act = lax.dot_general(
+        gout_ref[...], w_ref[...], (((1,), (1,)), ((), ())), preferred_element_type=F32
+    )
+    part = jnp.sum(grad_act * slope_ref[...], axis=0, keepdims=True)
+    slots[...] = jnp.zeros_like(slots)
+    for i in range(16):
+        slots[pl.ds(me ^ i, 1), :unit] = part[:, i * unit : (i + 1) * unit]
+    for kp in range(4):
+        out = send if kp % 2 else keep
+        for kz in range(4):
+            out[kp // 2 : kp // 2 + 1, 128 * kz : 128 * kz + 128] = slots[4 * kz + kp : 4 * kz + kp + 1, :]
+
+
+def fold_a_kernel(unit, keep_a, got, keep_g, got_g, send, own, send_g, own_g):
     two = 2 * unit
-    send[:two, :] = (keep_a[two:, :] + got[two : 2 * two, :].astype(F32)).astype(BF)
-    extra = got[2 * two :, :].astype(F32)
-    own_g[...] = jnp.zeros_like(own_g)
-    own_g[0:1, :] = keep_g[0:1, :] + (extra[0:1, :] + extra[1:2, :])
-    line = keep_g[1:2, :] + (extra[2:3, :] + extra[3:4, :])
-    send[two:, :] = stack_rows(split(line, 2), (16, line.shape[1])).astype(BF)
+    own_g[...] = keep_g[0:1, :] + got_g[0:1, :]
+    send_g[...] = keep_g[1:2, :] + got_g[1:2, :]
+    send[...] = (keep_a[two:, :] + got[two:, :].astype(F32)).astype(BF)
     own[...] = keep_a[:two, :] + got[:two, :].astype(F32)
 
 
@@ -244,17 +242,15 @@
     own[...] = keep_b[:two, :] + got[:two, :].astype(F32)
 
 
-def turn_a_kernel(unit, own, own_g, got, send1, mine, line_ref):
-    two = 2 * unit
+def turn_a_kernel(unit, own, got, own_g, got_g, send1, mine, line_ref):
     half = own.shape[1]
-    extra = got[two:, :].astype(F32)
-    line = own_g[0:1, :] + (extra[0:1, :] + extra[1:2, :])
-    send1[:unit, :] = (own[unit:, :] + got[unit:two, :].astype(F32)).astype(BF)
+    line = own_g[...] + got_g[...]
+    send1[:unit, :] = (own[unit:, :] + got[unit:, :].astype(F32)).astype(BF)
     send1[unit:, :] = jnp.zeros((16, half), BF)
     send1[unit:, :128] = stack_rows(split(line[:, 128:256], 2), (16, 128)).astype(BF)
     mine[...] = own[:unit, :] + got[:unit, :].astype(F32)
     line_ref[...] = jnp.zeros_like(line_ref)
-    line_ref[0:1, :] = line
+    line_ref[0:1, :512] = line
 
 
 def turn_b_kernel(unit, own, got, line_ref, send2, send3):
@@ -326,10 +322,18 @@
     own = call(
         pack_kernel,
         arr((unit + 16, half), BF),
-        [HBM, VMEM],
-        [pltpu.VMEM((unit, half), F32), pltpu.SemaphoreType.DMA],
+        [HBM, HBM],
+        [
+            pltpu.VMEM((unit, half), F32),
+            pltpu.VMEM((1, unit), F32),
+            pltpu.SemaphoreType.DMA,
+            pltpu.SemaphoreType.DMA,
+        ],
         byts=6 * unit * half,
-    )(master_weight, norm_gain.reshape(1, unit))
+    )(
+        pltpu.with_memory_space_constraint(master_weight, pltpu.HBM),
+        pltpu.with_memory_space_constraint(norm_gain.reshape(1, unit), pltpu.HBM),
+    )
     z1, z2, z3 = to(own, 4), to(own, 8), to(own, 12)
     wa, wb, tile = call(
         functools.partial(join_kernel, unit),
@@ -340,7 +344,7 @@
     wa1, wb1 = to(wa, 1), to(wb, 2)
     far = to(tile, 3)
     pair = call(pair_kernel, arr((four, half), BF), [VMEM] * 2 + [ANY], byts=16 * unit * half)
-    pair_a, pair_b = pair(wa, wa1, far), pair(wb, wb1, far)
+    pair_a, pair_b = pair(wa, wa1, tile), pair(wb, wb1, far)
     wa2, wb2 = to(pair_a, 2), to(pair_b, 1)
 
     other_latents, other_noise = across(latents), across(noise)
@@ -357,34 +361,42 @@
         byts=28 * both * width,
     )(coef, embed, tile, wa1, wb1, far, latents, noise, other_latents, other_noise, pair_a, pair_b)
 
-    send_a, send_b, keep_a, keep_b, keep_g = call(
+    send_a, send_b, keep_a, keep_b, mixing, gout = call(
         functools.partial(mix_kernel, 1.0 / math.sqrt(total_rows), unit),
         (
-            arr((four + 16, half), BF),
+            arr((four, half), BF),
             arr((four, half), BF),
             arr((four, half), F32),
             arr((four, half), F32),
-            arr((8, half), F32),
+            arr((width, half), BF),
+            arr((both, half), BF),
         ),
-        [VMEM] * 9,
-        [
-            pltpu.VMEM((width, half), BF),
-            pltpu.VMEM((width, half), F32),
-            pltpu.VMEM((both, half), BF),
-            pltpu.VMEM((16, 128), F32),
-        ],
-        flops=6 * both * width * half,
+        [VMEM] * 8,
+        [pltpu.VMEM((width, half), F32)],
+        flops=4 * both * width * half,
         byts=6 * both * width,
-    )(act, slope, diff, wa, wa1, wa2, wb, wb1, wb2)
+    )(act, diff, wa, wa1, wa2, wb, wb1, wb2)
 
     got_a, got_b = to(send_a, 1), to(send_b, 2)
-    send_a, own_a, own_g = call(
+    pair_line = arr((2, 512), F32)
+    thin_line = arr((1, 512), F32)
+    keep_g, send_g = call(
+        functools.partial(gain_kernel, unit),
+        (pair_line, pair_line),
+        [VMEM] * 3,
+        [pltpu.VMEM((16, 128), F32)],
+        flops=2 * both * width * half,
+        byts=6 * both * width,
+    )(gout, mixing, slope)
+    got_g = to(send_g, 1)
+    send_a, own_a, send_g, own_g = call(
         functools.partial(fold_a_kernel, unit),
-        (arr((two + 16, half), BF), arr((two, half), F32), arr((8, half), F32)),
-        [VMEM] * 3,
+        (arr((two, half), BF), arr((two, half), F32), thin_line, thin_line),
+        [VMEM] * 4,
         byts=8 * four * half,
-    )(keep_a, keep_g, got_a)
+    )(keep_a, got_a, keep_g, got_g)
     got_a = to(send_a, 2)
+    got_g = to(send_g, 2)
     send_b, own_b = call(
         functools.partial(fold_b_kernel, unit),
         (arr((two, half), BF), arr((two, half), F32)),
@@ -395,9 +407,9 @@
     send1, mine, line = call(
         functools.partial(turn_a_kernel, unit),
         (arr((unit + 16, half), BF), arr((unit, half), F32), arr((8, half), F32)),
-        [VMEM] * 3,
+        [VMEM] * 4,
         byts=8 * two * half,
-    )(own_a, own_g, got_a)
+    )(own_a, got_a, own_g, got_g)
     h1 = to(send1, 4)
     send2, send3 = call(
         functools.partial(turn_b_kernel, unit),

time: 70.7 us -> 68.1 us (0.963)
  waiting for transfers between devices: 34.7 us -> 30.6 us
  starting transfers between devices: 19.5 us -> 22.1 us
  local copies, waits for them, and re-layouts: 2.93 us -> 1.28 us
    ppermute x15 -> x17, waiting for transfers between devices: 33.3 us -> 29.1 us  [to(): return lax.ppermute(x, AXES, pairs)]
    ppermute x15 -> x17, starting transfers between devices: 19 us -> 21.5 us  [to(): return lax.ppermute(x, AXES, pairs)]
    pallas_call x4 -> x5, Pallas kernels: 0.22 us -> 2.55 us  [the longest x1 1.34 us: paired_body(): call(functools.partial(gain_kernel, unit), (pair_line, pair_line), [VMEM]...]
    unnamed x20 -> x16, local copies, waits for them, and re-layouts: 1.7 us -> 0.04 us
    pallas_call x1, Pallas kernels: 3.61 us -> 2.59 us  [paired_body(): call(functools.partial(mix_kernel, 1.0 / math.sqrt(total_rows), unit), (a...]
  transfers between devices with their start and end apart: 18 -> 20, of which waited for: 11 -> 13; matrix products, arithmetic and copies ran while one was open for 2% -> 2% of each run, Pallas kernels for 8% -> 10%
where the time goes in v4:
time: 68.1 us; the launch traced here: 67.9 us
  waiting for transfers between devices  30.6 us (45%)
  starting transfers between devices  22.1 us (32%)
  Pallas kernels  12.1 us (18%)
  between operations  1.66 us (2%)
  local copies, waits for them, and re-layouts  1.28 us (2%)
    ppermute x17, waiting for transfers between devices, to(): return lax.ppermute(x, AXES, pairs)  29.1 us
    ppermute x17, starting transfers between devices, to(): return lax.ppermute(x, AXES, pairs)  21.5 us
    pallas_call x1, Pallas kernels, paired_body(): call(functools.partial(act_kernel, unit), (arr((both, width), BF), arr((b...  5.38 us
    pallas_call x1, Pallas kernels, paired_body(): call(functools.partial(mix_kernel, 1.0 / math.sqrt(total_rows), unit), (a...  2.59 us
    ppermute x3, waiting for transfers between devices, across(): return lax.ppermute(x, AXES, pairs)  1.47 us
  transfers between devices with their start and end apart: 20, of which 13 were waited for; matrix products, arithmetic and copies ran while one was open for 2% of the time, Pallas kernels for 10%

profile of v4, /device:TPU:0, one launch (start us, length us, event | category | flops | bytes accessed | tf_op | source)
XLA Modules:
  0.0 67.9 jit_solution(3841872993207665158)
XLA Ops:
  0.7 1.1 %shard_map.136.own = bf16[96,640]{1,0:T(8,128)(2,1)S(1)} custom-call(f32[80,1280]{1,0:T(8,128)} %w.1, f32[1,80]{1,0:T(1,128)} %bitcast.7), custom_call_target="tpu_custom_call" | custom-call | bytes 307200 | tf_op jit(solution)/shard_map/pallas_call | solution.py:322
  1.7 5.1 %collective-permute-start.2 = (bf16[96,640]{1,0:T(8,128)(2,1)S(1)}, bf16[96,640]{1,0:T(8,128)(2,1)S(1)}, u32[]{:S(2)}, u32[]{:S(2)}) collective-permute-start(bf16[96,640]{1,0:T(8,128)(2,1)S(1)} %shard_map.136.own), channel_id=1, source_target_pairs={{0,24},{1,25},{2,26},{3,27},{4,28},{5,29},{6,30},{7,31},{8,16},{9,... | collective-permute-start | bytes 368648 | tf_op jit(solution)/shard_map/ppermute | solution.py:302
  7.5 3.6 %collective-permute-done.2.z3 = bf16[96,640]{1,0:T(8,128)(2,1)S(1)} collective-permute-done((bf16[96,640]{1,0:T(8,128)(2,1)S(1)}, bf16[96,640]{1,0:T(8,128)(2,1)S(1)}, u32[]{:S(2)}, u32[]{:S(2)}) %collective-permute-start.2) | collective-permute-done | bytes 122912 | tf_op jit(solution)/shard_map/ppermute | solution.py:302
  11.1 6.1 %collective-permute-done.1.z2 = bf16[96,640]{1,0:T(8,128)(2,1)S(1)} collective-permute-done((bf16[96,640]{1,0:T(8,128)(2,1)S(1)}, bf16[96,640]{1,0:T(8,128)(2,1)S(1)}, u32[]{:S(2)}, u32[]{:S(2)}) %collective-permute-start.1) | collective-permute-done | bytes 122912 | tf_op jit(solution)/shard_map/ppermute | solution.py:302
  17.3 1.6 %collective-permute-start.3 = (bf16[176,640]{1,0:T(8,128)(2,1)S(1)}, bf16[176,640]{1,0:T(8,128)(2,1)S(1)}, u32[]{:S(2)}, u32[]{:S(2)}) collective-permute-start(bf16[176,640]{1,0:T(8,128)(2,1)S(1)} %get-tuple-element.38.first.wa), channel_id=1, source_target_pairs={{0,2},{1,3},{2,0},{3,1},{4,6},{5,7},{6,4},{7,5},{8,10},{9,11},{10,... | collective-permute-start | bytes 675848 | tf_op jit(solution)/shard_map/ppermute | solution.py:302
  18.8 1.5 %collective-permute-start.4 = (bf16[176,640]{1,0:T(8,128)(2,1)S(1)}, bf16[176,640]{1,0:T(8,128)(2,1)S(1)}, u32[]{:S(2)}, u32[]{:S(2)}) collective-permute-start(bf16[176,640]{1,0:T(8,128)(2,1)S(1)} %get-tuple-element.39.first.wb), channel_id=1, source_target_pairs={{0,4},{1,5},{2,6},{3,7},{4,0},{5,1},{6,2},{7,3},{8,12},{9,13},{10,... | collective-permute-start | bytes 675848 | tf_op jit(solution)/shard_map/ppermute | solution.py:302
  21.3 1.2 %dynamic_slice.3 = s32[1]{0:T(128)} dynamic-slice(s32[16]{0:T(128)} %param.11, s32[]{:T(128)S(6)} %select_n.9), dynamic_slice_sizes={1} | dynamic-slice | bytes 12 | tf_op jit(solution)/shard_map/dynamic_slice | solution.py:351
  24.2 1.6 %collective-permute-start.8 = (bf16[320,640]{1,0:T(8,128)(2,1)S(1)}, bf16[320,640]{1,0:T(8,128)(2,1)S(1)}, u32[]{:S(2)}, u32[]{:S(2)}) collective-permute-start(bf16[320,640]{1,0:T(8,128)(2,1)S(1)} %shard_map.138.after_a), channel_id=1, source_target_pairs={{0,4},{1,5},{2,6},{3,7},{4,0},{5,1},{6,2},{7,3},{8,12},{9,13},{10,... | collective-permute-start | bytes 1228808 | tf_op jit(solution)/shard_map/ppermute | solution.py:302
  25.8 1.6 %collective-permute-start.9 = (bf16[320,640]{1,0:T(8,128)(2,1)S(1)}, bf16[320,640]{1,0:T(8,128)(2,1)S(1)}, u32[]{:S(2)}, u32[]{:S(2)}) collective-permute-start(bf16[320,640]{1,0:T(8,128)(2,1)S(1)} %shard_map.139.after_b), channel_id=1, source_target_pairs={{0,2},{1,3},{2,0},{3,1},{4,6},{5,7},{6,4},{7,5},{8,10},{9,11},{10,... | collective-permute-start | bytes 1228808 | tf_op jit(solution)/shard_map/ppermute | solution.py:302
  27.6 5.4 %shard_map.140 = (bf16[512,1280]{1,0:T(8,128)(2,1)S(1)}, f32[512,1280]{1,0:T(8,128)S(1)}, f32[512,640]{1,0:T(8,128)S(1)}) custom-call(f32[2]{0:T(128)S(1)} %pad_maximum_fusion.1.coef_ref, f32[1,1280]{1,0:T(1,128)S(1)} %pad_maximum_fusion.embed_ref, bf16[16,640]{1,0:T(8,128)(2,1)S(1)} %get-tuple-element.37.after.t0, ...), custom_call_target="tpu_custom_call" | custom-call | bytes 18350080 | tf_op jit(solution)/shard_map/pallas_call | solution.py:356
  33.0 1.6 %collective-permute-done.8.wa2 = bf16[320,640]{1,0:T(8,128)(2,1)S(1)} collective-permute-done((bf16[320,640]{1,0:T(8,128)(2,1)S(1)}, bf16[320,640]{1,0:T(8,128)(2,1)S(1)}, u32[]{:S(2)}, u32[]{:S(2)}) %collective-permute-start.8) | collective-permute-done | bytes 409632 | tf_op jit(solution)/shard_map/ppermute | solution.py:302
  34.6 1.7 %collective-permute-done.9.wb2 = bf16[320,640]{1,0:T(8,128)(2,1)S(1)} collective-permute-done((bf16[320,640]{1,0:T(8,128)(2,1)S(1)}, bf16[320,640]{1,0:T(8,128)(2,1)S(1)}, u32[]{:S(2)}, u32[]{:S(2)}) %collective-permute-start.9) | collective-permute-done | bytes 409632 | tf_op jit(solution)/shard_map/ppermute | solution.py:302
  36.3 2.6 %shard_map.141 = (bf16[320,640]{1,0:T(8,128)(2,1)S(1)}, bf16[320,640]{1,0:T(8,128)(2,1)S(1)}, f32[320,640]{1,0:T(8,128)S(1)}, f32[320,640]{1,0:T(8,128)S(1)}, bf...) custom-call(bf16[512,1280]{1,0:T(8,128)(2,1)S(1)} %get-tuple-element.40.act_ref, ...), custom_call_target="tpu_custom_call" | custom-call | flops 1677721600 | bytes 3932160 | tf_op jit(solution)/shard_map/pallas_call | solution.py:364
  38.9 1.2 %collective-permute-start.10 = (bf16[320,640]{1,0:T(8,128)(2,1)S(1)}, bf16[320,640]{1,0:T(8,128)(2,1)S(1)}, u32[]{:S(2)}, u32[]{:S(2)}) collective-permute-start(bf16[320,640]{1,0:T(8,128)(2,1)S(1)} %get-tuple-element.43), channel_id=1, source_target_pairs={{0,2},{1,3},{2,0},{3,1},{4,6},{5,7},{6,4},{7,5},{8,10},{9,11},{10,... | collective-permute-start | bytes 1228808 | tf_op jit(solution)/shard_map/ppermute | solution.py:302
  40.6 1.3 %shard_map.142 = (f32[2,512]{1,0:T(2,128)S(1)}, f32[2,512]{1,0:T(2,128)S(1)}) custom-call(bf16[512,640]{1,0:T(8,128)(2,1)S(1)} %get-tuple-element.44.gout_ref, bf16[1280,640]{1,0:T(8,128)(2,1)S(1)} %get-tuple-element.45.w_ref, f32[512,1280]{1,0:T(8,128)S(1)} %get-tuple-element.46.slope_ref), custom_call_target="tpu_custom_call" | custom-call | flops 838860800 | bytes 3932160 | tf_op jit(solution)/shard_map/pallas_call | solution.py:383
  42.9 5.6 %collective-permute-done.11.got_g = f32[2,512]{1,0:T(2,128)S(1)} collective-permute-done((f32[2,512]{1,0:T(2,128)S(1)}, f32[2,512]{1,0:T(2,128)S(1)}, u32[]{:S(2)}, u32[]{:S(2)}) %collective-permute-start.11) | collective-permute-done | bytes 4128 | tf_op jit(solution)/shard_map/ppermute | solution.py:302
  49.6 1.8 %collective-permute-start.16 = (bf16[160,640]{1,0:T(8,128)(2,1)S(1)}, bf16[160,640]{1,0:T(8,128)(2,1)S(1)}, u32[]{:S(2)}, u32[]{:S(2)}) collective-permute-start(bf16[160,640]{1,0:T(8,128)(2,1)S(1)} %get-tuple-element.59), channel_id=1, source_target_pairs={{0,2},{1,3},{2,0},{3,1},{4,6},{5,7},{6,4},{7,5},{8,10},{9,11},{10,... | collective-permute-start | bytes 614408 | tf_op jit(solution)/shard_map/ppermute | solution.py:302
  51.7 3.3 %collective-permute-done.13.got_g = f32[1,512]{1,0:T(1,128)S(1)} collective-permute-done((f32[1,512]{1,0:T(1,128)S(1)}, f32[1,512]{1,0:T(1,128)S(1)}, u32[]{:S(2)}, u32[]{:S(2)}) %collective-permute-start.13) | collective-permute-done | bytes 2080 | tf_op jit(solution)/shard_map/ppermute | solution.py:302
  55.5 2.7 %collective-permute-start.17 = (bf16[96,640]{1,0:T(8,128)(2,1)S(1)}, bf16[96,640]{1,0:T(8,128)(2,1)S(1)}, u32[]{:S(2)}, u32[]{:S(2)}) collective-permute-start(bf16[96,640]{1,0:T(8,128)(2,1)S(1)} %get-tuple-element.60), channel_id=1, source_target_pairs={{0,16},{1,17},{2,18},{3,19},{4,20},{5,21},{6,22},{7,23},{8,24},{9,... | collective-permute-start | bytes 368648 | tf_op jit(solution)/shard_map/ppermute | solution.py:302
  58.1 1.5 %collective-permute-start.18 = (bf16[96,640]{1,0:T(8,128)(2,1)S(1)}, bf16[96,640]{1,0:T(8,128)(2,1)S(1)}, u32[]{:S(2)}, u32[]{:S(2)}) collective-permute-start(bf16[96,640]{1,0:T(8,128)(2,1)S(1)} %get-tuple-element.61), channel_id=1, source_target_pairs={{0,24},{1,25},{2,26},{3,27},{4,28},{5,29},{6,30},{7,31},{8,16},{9,... | collective-permute-start | bytes 368648 | tf_op jit(solution)/shard_map/ppermute | solution.py:302
  59.7 2.4 %collective-permute-done.14.h1 = bf16[96,640]{1,0:T(8,128)(2,1)S(1)} collective-permute-done((bf16[96,640]{1,0:T(8,128)(2,1)S(1)}, bf16[96,640]{1,0:T(8,128)(2,1)S(1)}, u32[]{:S(2)}, u32[]{:S(2)}) %collective-permute-start.14) | collective-permute-done | bytes 122912 | tf_op jit(solution)/shard_map/ppermute | solution.py:302
  63.0 2.0 %collective-permute-done.18.h3 = bf16[96,640]{1,0:T(8,128)(2,1)S(1)} collective-permute-done((bf16[96,640]{1,0:T(8,128)(2,1)S(1)}, bf16[96,640]{1,0:T(8,128)(2,1)S(1)}, u32[]{:S(2)}, u32[]{:S(2)}) %collective-permute-start.18) | collective-permute-done | bytes 122912 | tf_op jit(solution)/shard_map/ppermute | solution.py:302
  65.1 1.5 %collective-permute-done.19.theirs = f32[88,640]{1,0:T(8,128)S(1)} collective-permute-done((f32[88,640]{1,0:T(8,128)S(1)}, f32[88,640]{1,0:T(8,128)S(1)}, u32[]{:S(2)}, u32[]{:S(2)}) %collective-permute-start.19) | collective-permute-done | bytes 225312 | tf_op jit(solution)/shard_map/ppermute | solution.py:306
  66.6 1.3 %shard_map.148 = (f32[80,1280]{1,0:T(8,128)}, f32[80,1280]{1,0:T(8,128)}, f32[80,1280]{1,0:T(8,128)}, f32[1,80]{1,0:T(1,128)}, f32[1,80]{1,0:T(1,128)}, /*index=5*/f32[1,80]{1,0:T(1,128)}) custom-call(f32[88,640]{1,0:T(8,128)S(1)} %shard_map.147.mine, f32[88,640]{1,0:T(8,128)S(1)} %collective-permute-done.19.theirs, f32[80,1280]{1,0:T(8,128)S(1)} %copy-done, ...), custom_call_target="tpu_custom_call" | custom-call | bytes 2457600 | tf_op jit(solution)/shard_map/pallas_call | solution.py:430
  (49 shorter events, 7.0 us)
Async XLA Ops:
  0.6 26.9 %copy-start.1 = (bf16[256,1280]{1,0:T(8,128)(2,1)S(1)}, bf16[256,1280]{1,0:T(8,128)(2,1)}, u32[]{:S(2)}) copy-start(bf16[256,1280]{1,0:T(8,128)(2,1)} %l0.1) | copy-start | bytes 1966084
  0.6 26.9 %copy-start.2 = (bf16[256,1280]{1,0:T(8,128)(2,1)S(1)}, bf16[256,1280]{1,0:T(8,128)(2,1)}, u32[]{:S(2)}) copy-start(bf16[256,1280]{1,0:T(8,128)(2,1)} %n0.1) | copy-start | bytes 1966084
  1.7 9.4 %collective-permute-start.2 = (bf16[96,640]{1,0:T(8,128)(2,1)S(1)}, bf16[96,640]{1,0:T(8,128)(2,1)S(1)}, u32[]{:S(2)}, u32[]{:S(2)}) collective-permute-start(bf16[96,640]{1,0:T(8,128)(2,1)S(1)} %shard_map.136.own), channel_id=1, source_target_pairs={{0,24},{1,25},{2,26},{3,27},{4,28},{5,29},{6,30},{7,31},{8,16},{9,... | collective-permute-start | bytes 368648 | tf_op jit(solution)/shard_map/ppermute | solution.py:302
  6.9 10.4 %collective-permute-start.1 = (bf16[96,640]{1,0:T(8,128)(2,1)S(1)}, bf16[96,640]{1,0:T(8,128)(2,1)S(1)}, u32[]{:S(2)}, u32[]{:S(2)}) collective-permute-start(bf16[96,640]{1,0:T(8,128)(2,1)S(1)} %shard_map.136.own), channel_id=1, source_target_pairs={{0,16},{1,17},{2,18},{3,19},{4,20},{5,21},{6,22},{7,23},{8,24},{9,... | collective-permute-start | bytes 368648 | tf_op jit(solution)/shard_map/ppermute | solution.py:302
  6.9 10.4 %collective-permute-start = (bf16[96,640]{1,0:T(8,128)(2,1)S(1)}, bf16[96,640]{1,0:T(8,128)(2,1)S(1)}, u32[]{:S(2)}, u32[]{:S(2)}) collective-permute-start(bf16[96,640]{1,0:T(8,128)(2,1)S(1)} %shard_map.136.own), channel_id=1, source_target_pairs={{0,8},{1,9},{2,10},{3,11},{4,12},{5,13},{6,14},{7,15},{8,0},{9,1},... | collective-permute-start | bytes 368648 | tf_op jit(solution)/shard_map/ppermute | solution.py:302
  17.3 6.9 %collective-permute-start.3 = (bf16[176,640]{1,0:T(8,128)(2,1)S(1)}, bf16[176,640]{1,0:T(8,128)(2,1)S(1)}, u32[]{:S(2)}, u32[]{:S(2)}) collective-permute-start(bf16[176,640]{1,0:T(8,128)(2,1)S(1)} %get-tuple-element.38.first.wa), channel_id=1, source_target_pairs={{0,2},{1,3},{2,0},{3,1},{4,6},{5,7},{6,4},{7,5},{8,10},{9,11},{10,... | collective-permute-start | bytes 675848 | tf_op jit(solution)/shard_map/ppermute | solution.py:302
  18.8 6.9 %collective-permute-start.4 = (bf16[176,640]{1,0:T(8,128)(2,1)S(1)}, bf16[176,640]{1,0:T(8,128)(2,1)S(1)}, u32[]{:S(2)}, u32[]{:S(2)}) collective-permute-start(bf16[176,640]{1,0:T(8,128)(2,1)S(1)} %get-tuple-element.39.first.wb), channel_id=1, source_target_pairs={{0,4},{1,5},{2,6},{3,7},{4,0},{5,1},{6,2},{7,3},{8,12},{9,13},{10,... | collective-permute-start | bytes 675848 | tf_op jit(solution)/shard_map/ppermute | solution.py:302
  20.4 7.2 %collective-permute-start.6 = (bf16[256,1280]{1,0:T(8,128)(2,1)}, bf16[256,1280]{1,0:T(8,128)(2,1)S(1)}, u32[]{:S(2)}, u32[]{:S(2)}) collective-permute-start(bf16[256,1280]{1,0:T(8,128)(2,1)} %l0.1), channel_id=1, source_target_pairs={{0,1},{1,0},{2,3},{3,2},{4,5},{5,4},{6,7},{7,6},{8,9},{9,8},{10,11... | collective-permute-start | bytes 1966088 | tf_op jit(solution)/shard_map/ppermute | solution.py:306
  20.4 7.2 %collective-permute-start.7 = (bf16[256,1280]{1,0:T(8,128)(2,1)}, bf16[256,1280]{1,0:T(8,128)(2,1)S(1)}, u32[]{:S(2)}, u32[]{:S(2)}) collective-permute-start(bf16[256,1280]{1,0:T(8,128)(2,1)} %n0.1), channel_id=1, source_target_pairs={{0,1},{1,0},{2,3},{3,2},{4,5},{5,4},{6,7},{7,6},{8,9},{9,8},{10,11... | collective-permute-start | bytes 1966088 | tf_op jit(solution)/shard_map/ppermute | solution.py:306
  20.9 4.9 %collective-permute-start.5 = (bf16[16,640]{1,0:T(8,128)(2,1)S(1)}, bf16[16,640]{1,0:T(8,128)(2,1)}, u32[]{:S(2)}, u32[]{:S(2)}) collective-permute-start(bf16[16,640]{1,0:T(8,128)(2,1)S(1)} %get-tuple-element.37.after.t0), channel_id=1, source_target_pairs={{0,6},{1,7},{2,4},{3,5},{4,2},{5,3},{6,0},{7,1},{8,14},{9,15},{10,... | collective-permute-start | bytes 61448 | tf_op jit(solution)/shard_map/ppermute | solution.py:302
  24.2 10.4 %collective-permute-start.8 = (bf16[320,640]{1,0:T(8,128)(2,1)S(1)}, bf16[320,640]{1,0:T(8,128)(2,1)S(1)}, u32[]{:S(2)}, u32[]{:S(2)}) collective-permute-start(bf16[320,640]{1,0:T(8,128)(2,1)S(1)} %shard_map.138.after_a), channel_id=1, source_target_pairs={{0,4},{1,5},{2,6},{3,7},{4,0},{5,1},{6,2},{7,3},{8,12},{9,13},{10,... | collective-permute-start | bytes 1228808 | tf_op jit(solution)/shard_map/ppermute | solution.py:302
  25.8 10.5 %collective-permute-start.9 = (bf16[320,640]{1,0:T(8,128)(2,1)S(1)}, bf16[320,640]{1,0:T(8,128)(2,1)S(1)}, u32[]{:S(2)}, u32[]{:S(2)}) collective-permute-start(bf16[320,640]{1,0:T(8,128)(2,1)S(1)} %shard_map.139.after_b), channel_id=1, source_target_pairs={{0,2},{1,3},{2,0},{3,1},{4,6},{5,7},{6,4},{7,5},{8,10},{9,11},{10,... | collective-permute-start | bytes 1228808 | tf_op jit(solution)/shard_map/ppermute | solution.py:302
  38.9 9.6 %collective-permute-start.10 = (bf16[320,640]{1,0:T(8,128)(2,1)S(1)}, bf16[320,640]{1,0:T(8,128)(2,1)S(1)}, u32[]{:S(2)}, u32[]{:S(2)}) collective-permute-start(bf16[320,640]{1,0:T(8,128)(2,1)S(1)} %get-tuple-element.43), channel_id=1, source_target_pairs={{0,2},{1,3},{2,0},{3,1},{4,6},{5,7},{6,4},{7,5},{8,10},{9,11},{10,... | collective-permute-start | bytes 1228808 | tf_op jit(solution)/shard_map/ppermute | solution.py:302
  40.1 9.4 %collective-permute-start.15 = (bf16[320,640]{1,0:T(8,128)(2,1)S(1)}, bf16[320,640]{1,0:T(8,128)(2,1)S(1)}, u32[]{:S(2)}, u32[]{:S(2)}) collective-permute-start(bf16[320,640]{1,0:T(8,128)(2,1)S(1)} %get-tuple-element.57), channel_id=1, source_target_pairs={{0,4},{1,5},{2,6},{3,7},{4,0},{5,1},{6,2},{7,3},{8,12},{9,13},{10,... | collective-permute-start | bytes 1228808 | tf_op jit(solution)/shard_map/ppermute | solution.py:302
  42.0 6.5 %collective-permute-start.11 = (f32[2,512]{1,0:T(2,128)S(1)}, f32[2,512]{1,0:T(2,128)S(1)}, u32[]{:S(2)}, u32[]{:S(2)}) collective-permute-start(f32[2,512]{1,0:T(2,128)S(1)} %get-tuple-element.48), channel_id=1, source_target_pairs={{0,2},{1,3},{2,0},{3,1},{4,6},{5,7},{6,4},{7,5},{8,10},{9,11},{10,... | collective-permute-start | bytes 12296 | tf_op jit(solution)/shard_map/ppermute | solution.py:302
  48.6 6.5 %collective-permute-start.12 = (bf16[160,640]{1,0:T(8,128)(2,1)S(1)}, bf16[160,640]{1,0:T(8,128)(2,1)S(1)}, u32[]{:S(2)}, u32[]{:S(2)}) collective-permute-start(bf16[160,640]{1,0:T(8,128)(2,1)S(1)} %get-tuple-element.50), channel_id=1, source_target_pairs={{0,4},{1,5},{2,6},{3,7},{4,0},{5,1},{6,2},{7,3},{8,12},{9,13},{10,... | collective-permute-start | bytes 614408 | tf_op jit(solution)/shard_map/ppermute | solution.py:302
  49.5 17.0 %copy-start.6 = (f32[80]{0:T(128)S(1)}, f32[80]{0:T(128)}, u32[]{:S(2)}) copy-start(f32[80]{0:T(128)} %param.16) | copy-start | bytes 964
  49.5 17.0 %copy-start.7 = (f32[80]{0:T(128)S(1)}, f32[80]{0:T(128)}, u32[]{:S(2)}) copy-start(f32[80]{0:T(128)} %param.17) | copy-start | bytes 964
  49.6 5.8 %collective-permute-start.16 = (bf16[160,640]{1,0:T(8,128)(2,1)S(1)}, bf16[160,640]{1,0:T(8,128)(2,1)S(1)}, u32[]{:S(2)}, u32[]{:S(2)}) collective-permute-start(bf16[160,640]{1,0:T(8,128)(2,1)S(1)} %get-tuple-element.59), channel_id=1, source_target_pairs={{0,2},{1,3},{2,0},{3,1},{4,6},{5,7},{6,4},{7,5},{8,10},{9,11},{10,... | collective-permute-start | bytes 614408 | tf_op jit(solution)/shard_map/ppermute | solution.py:302
  51.4 3.6 %collective-permute-start.13 = (f32[1,512]{1,0:T(1,128)S(1)}, f32[1,512]{1,0:T(1,128)S(1)}, u32[]{:S(2)}, u32[]{:S(2)}) collective-permute-start(f32[1,512]{1,0:T(1,128)S(1)} %get-tuple-element.52), channel_id=1, source_target_pairs={{0,4},{1,5},{2,6},{3,7},{4,0},{5,1},{6,2},{7,3},{8,12},{9,13},{10,... | collective-permute-start | bytes 6152 | tf_op jit(solution)/shard_map/ppermute | solution.py:302
  55.1 6.9 %collective-permute-start.14 = (bf16[96,640]{1,0:T(8,128)(2,1)S(1)}, bf16[96,640]{1,0:T(8,128)(2,1)S(1)}, u32[]{:S(2)}, u32[]{:S(2)}) collective-permute-start(bf16[96,640]{1,0:T(8,128)(2,1)S(1)} %get-tuple-element.55), channel_id=1, source_target_pairs={{0,8},{1,9},{2,10},{3,11},{4,12},{5,13},{6,14},{7,15},{8,0},{9,1},... | collective-permute-start | bytes 368648 | tf_op jit(solution)/shard_map/ppermute | solution.py:302
  55.5 7.5 %collective-permute-start.17 = (bf16[96,640]{1,0:T(8,128)(2,1)S(1)}, bf16[96,640]{1,0:T(8,128)(2,1)S(1)}, u32[]{:S(2)}, u32[]{:S(2)}) collective-permute-start(bf16[96,640]{1,0:T(8,128)(2,1)S(1)} %get-tuple-element.60), channel_id=1, source_target_pairs={{0,16},{1,17},{2,18},{3,19},{4,20},{5,21},{6,22},{7,23},{8,24},{9,... | collective-permute-start | bytes 368648 | tf_op jit(solution)/shard_map/ppermute | solution.py:302
  58.1 6.8 %collective-permute-start.18 = (bf16[96,640]{1,0:T(8,128)(2,1)S(1)}, bf16[96,640]{1,0:T(8,128)(2,1)S(1)}, u32[]{:S(2)}, u32[]{:S(2)}) collective-permute-start(bf16[96,640]{1,0:T(8,128)(2,1)S(1)} %get-tuple-element.61), channel_id=1, source_target_pairs={{0,24},{1,25},{2,26},{3,27},{4,28},{5,29},{6,30},{7,31},{8,16},{9,... | collective-permute-start | bytes 368648 | tf_op jit(solution)/shard_map/ppermute | solution.py:302
  65.0 1.5 %collective-permute-start.19 = (f32[88,640]{1,0:T(8,128)S(1)}, f32[88,640]{1,0:T(8,128)S(1)}, u32[]{:S(2)}, u32[]{:S(2)}) collective-permute-start(f32[88,640]{1,0:T(8,128)S(1)} %shard_map.147.mine), channel_id=1, source_target_pairs={{0,1},{1,0},{2,3},{3,2},{4,5},{5,4},{6,7},{7,6},{8,9},{9,8},{10,11... | collective-permute-start | bytes 675848 | tf_op jit(solution)/shard_map/ppermute | solution.py:306
  (4 other events, 68.1 us)
